TPU v7x, 512 devices: a whole 4x8x8 slice. The times are simulated.
512 devices in a mesh: wide: 64 (over y, z), narrow: 8 (over x, core).
Axes of the slice: x: 4, y: 8, z: 8, core: 2. Of those that a mesh axis runs over, the one named last changes fastest.
Arguments:
- amplitudes: bfloat16 [1024, 1024, 128], P('wide', 'narrow'), may hold values from -6 to 6
- send_list: int32 [64, 128], P('wide'), may hold values from 0 to 15
- tile_positions: int32 [512, 16], P('wide', 'narrow'), may hold values from 0 to 127
- integrals: bfloat16 [512, 16, 128, 128], P('wide', 'narrow'), may hold values from -0.125 to 0.125
Outputs:
- ladder: bfloat16 [512, 1024, 128], P('wide', 'narrow')
All inputs are finite; a program needn't handle non-finite values.
Results may differ from a plain program's by a relative error of at most 0.001.
Values may be sent and summed in bfloat16 or wider, within the bound.
A program may use at most 64 MiB of HBM per device.

v0:
```python
import jax
import jax.numpy as jnp
from jax import lax
from jax.sharding import PartitionSpec as P


def on_device(amplitudes, send_list, tile_positions, integrals):
    outgoing = amplitudes[send_list[0]]
    tiles_dev = integrals.shape[0]
    received = lax.all_to_all(outgoing, "wide", split_axis=0, concat_axis=0, tiled=True)
    start_sum = jnp.zeros((tiles_dev, received.shape[1], integrals.shape[3]), jnp.float32)
    blocks = lax.all_gather(integrals, "narrow", axis=1, tiled=True)
    places = lax.all_gather(tile_positions, "narrow", axis=1, tiled=True)
    picked = received[places]
    total = start_sum + jnp.einsum(
        "xmpt,xmts->xps", picked, blocks, preferred_element_type=jnp.float32
    )
    return total.astype(jnp.bfloat16)


def solution(mesh):
    placed = (
        P("wide", "narrow", None),
        P("wide", None),
        P("wide", "narrow"),
        P("wide", "narrow", None, None),
    )
    return jax.shard_map(
        on_device, mesh=mesh, in_specs=placed, out_specs=P("wide", "narrow", None), check_vma=False
    )
```

profile of v0, /device:TPU:74, one launch (start us, length us, event | category | flops | bytes accessed | tf_op | source)
XLA Modules:
  0.0 183.3 jit_solution(16691365258464274699)
XLA Ops:
  6.5 0.0 copy-start
  6.5 0.7 fusion.1
  7.3 0.3 copy-done
  7.6 3.1 %gather_fusion = bf16[128,128,128]{2,1,0:T(8,128)(2,1)} fusion(bf16[16,128,128]{2,1,0:T(8,128)(2,1)S(1)} %copy-done, s32[1024]{0:T(1024)S(1)} %pad_clamp_fusion.1), kind=kCustom, calls=%fused_computation | custom fusion | bytes 8389120 | tf_op jit(solution)/shard_map/gather | solution.py:8
  10.6 0.0 copy-start.1
  10.6 16.0 %all-to-all-start = ((bf16[128,128,128]{2,1,0:T(8,128)(2,1)}), bf16[128,128,128]{2,1,0:T(8,128)(2,1)}, u32[]{:S(2)}, u32[]{:S(2)}) async-start(bf16[128,128,128]{2,1,0:T(8,128)(2,1)} %gather_fusion), calls=%async_computation | async-start | bytes 8388608 | tf_op jit(solution)/shard_map/all_to_all | solution.py:10
  26.7 0.0 all-gather.3.cloned.1.call-start
  26.7 0.7 all-gather.3.cloned.1.call-update
  27.4 0.0 copy-done.1
  27.4 8.7 %all-gather = s32[8,2,8]{2,1,0:T(2,128)S(1)} all-gather(s32[1,2,8]{2,1,0:T(2,128)S(1)} %bitcast.20), channel_id=1, replica_groups=mesh['wide'=64,'narrow'=8] {'narrow'}, dimensions={0}, use_global_device_ids=true | all-gather | bytes 576 | tf_op jit(solution)/shard_map/all_gather | solution.py:13
  36.1 0.1 copy.6
  36.2 0.1 reshape.38
  36.2 129.6 %all-to-all-done = bf16[128,128,128]{2,1,0:T(8,128)(2,1)} async-done(((bf16[128,128,128]{2,1,0:T(8,128)(2,1)}), bf16[128,128,128]{2,1,0:T(8,128)(2,1)}, u32[]{:S(2)}, u32[]{:S(2)}) %all-to-all-start) | async-done | bytes 4194336 | tf_op jit(solution)/shard_map/all_to_all | solution.py:10
  165.8 5.2 %gather_fusion.1 = bf16[128,128,128]{2,1,0:T(8,128)(2,1)} fusion(bf16[128,128,128]{2,1,0:T(8,128)(2,1)} %all-to-all-done, s32[1024]{0:T(1024)S(1)} %pad_clamp_fusion), kind=kCustom, calls=%fused_computation.1 | custom fusion | bytes 8389120 | tf_op jit(solution)/shard_map/gather | solution.py:14
  171.1 0.0 all-gather.3.cloned.1.call-done
  171.1 5.4 %fusion = bf16[8,128,128]{2,1,0:T(8,128)(2,1)} fusion(bf16[8,16,128,128]{3,2,1,0:T(8,128)(2,1)} %bitcast.18, bf16[8,16,128,128]{3,2,1,0:T(8,128)(2,1)} %all-gather.3.cloned.1.call-done), kind=kOutput, calls=%fused_computation.3 | convolution fusion | flops 537001984 | bytes 8650752 | tf_op jit(solution)/shard_map/xmpt,xmts->xps/dot_general | solution.py:15
  (3 shorter events, 0.0 us)
Async XLA Ops:
  6.5 1.1 copy-start
  10.6 16.7 %copy-start.1 = (s32[8,2]{0,1:T(2,128)S(1)}, s32[8,2]{0,1:T(2,128)}, u32[]{:S(2)}) copy-start(s32[8,2]{0,1:T(2,128)} %param.6) | copy-start | bytes 196
  10.6 155.2 %all-to-all-start = ((bf16[128,128,128]{2,1,0:T(8,128)(2,1)}), bf16[128,128,128]{2,1,0:T(8,128)(2,1)}, u32[]{:S(2)}, u32[]{:S(2)}) async-start(bf16[128,128,128]{2,1,0:T(8,128)(2,1)} %gather_fusion), calls=%async_computation | async-start | bytes 8388608 | tf_op jit(solution)/shard_map/all_to_all | solution.py:10
  26.7 144.4 %all-gather.3.cloned.1.call-start = ((), (), s32[]{:S(2)}) async-start(), calls=%async_computation.1 | async-start | bytes 4718592 | tf_op jit(solution)/shard_map/all_gather | solution.py:12
Sparse Core Ops, SparseCore 0:
  29.6 37.2 all-gather.2
where the time goes:
time: 184 us; the launch traced here: 183 us
  waiting for transfers between devices  130 us (71%)
  starting transfers between devices  16 us (9%)
  between operations  13.4 us (7%)
  local copies, waits for them, and re-layouts  8.78 us (5%)
  blocking collectives  8.68 us (5%)
  matrix products  5.41 us (3%)
    all_to_all x1, waiting for transfers between devices, on_device(): lax.all_to_all(outgoing, 'wide', split_axis=0, concat_axis=0, tiled=True)  130 us
    all_to_all x1, starting transfers between devices, on_device(): lax.all_to_all(outgoing, 'wide', split_axis=0, concat_axis=0, tiled=True)  16 us
    all_gather x1, blocking collectives, on_device(): places = lax.all_gather(tile_positions, 'narrow', axis=1, tiled=True)  8.68 us
    dot_general x1, matrix products, on_device(): jnp.einsum('xmpt,xmts->xps', picked, blocks, preferred_element_type=jnp.f...  5.41 us
    gather x1, local copies, waits for them, and re-layouts, on_device(): picked = received[places]  5.24 us
  transfers between devices with their start and end apart: 2, of which 1 were waited for; matrix products, arithmetic and copies ran while one was open for 3% of the time, Pallas kernels for 0%

commit v1 on v0

v1 whole, which is shorter than its diff:
```python
import functools

import jax
import jax.numpy as jnp
from jax import lax
from jax.experimental import pallas as pl
from jax.experimental.pallas import tpu as pltpu
from jax.sharding import PartitionSpec as P

MESH = pl.DeviceIdType.MESH


def exchange_kernel(n_wide, cap, out_hbm, recv_hbm, send_sem, recv_sem, local_sem):
    me = lax.axis_index("wide")
    nar = lax.axis_index("narrow")

    barrier = pltpu.get_barrier_semaphore()

    def greet(i, c):
        peer = lax.rem(me + i, n_wide)
        pl.semaphore_signal(barrier, 1, device_id=(peer, nar), device_id_type=MESH)
        return c

    lax.fori_loop(1, n_wide, greet, 0)
    pl.semaphore_wait(barrier, n_wide - 1)

    def block(ref, j):
        return ref.at[pl.ds(pl.multiple_of(j * cap, cap), cap)]

    local = pltpu.make_async_copy(block(out_hbm, me), block(recv_hbm, me), local_sem)
    local.start()

    def remote(peer, src_owner):
        return pltpu.make_async_remote_copy(
            src_ref=block(out_hbm, peer),
            dst_ref=block(recv_hbm, src_owner),
            send_sem=send_sem.at[peer],
            recv_sem=recv_sem.at[src_owner],
            device_id=(peer, nar),
            device_id_type=MESH,
        )

    def send(i, c):
        peer = lax.rem(me + i, n_wide)
        remote(peer, me).start()
        return c

    lax.fori_loop(1, n_wide, send, 0)

    def finish(i, c):
        peer = lax.rem(me + i, n_wide)
        remote(peer, me).wait_send()
        owner = lax.rem(me + n_wide - i, n_wide)
        remote(owner, owner).wait_recv()
        return c

    lax.fori_loop(1, n_wide, finish, 0)
    local.wait()


def exchange(outgoing, n_wide, cap):
    return pl.pallas_call(
        functools.partial(exchange_kernel, n_wide, cap),
        out_shape=jax.ShapeDtypeStruct(outgoing.shape, outgoing.dtype),
        in_specs=[pl.BlockSpec(memory_space=pl.ANY)],
        out_specs=pl.BlockSpec(memory_space=pl.ANY),
        scratch_shapes=[
            pltpu.SemaphoreType.DMA((n_wide,)),
            pltpu.SemaphoreType.DMA((n_wide,)),
            pltpu.SemaphoreType.DMA,
        ],
        compiler_params=pltpu.CompilerParams(collective_id=0, has_side_effects=True),
    )(outgoing)


def on_device(n_wide, amplitudes, send_list, tile_positions, integrals):
    cap = send_list.shape[1] // n_wide
    outgoing = amplitudes[send_list[0]]
    received = exchange(outgoing, n_wide, cap)
    start_sum = jnp.zeros((integrals.shape[0], received.shape[1], integrals.shape[3]), jnp.float32)
    blocks = lax.all_gather(integrals, "narrow", axis=1, tiled=True)
    places = lax.all_gather(tile_positions, "narrow", axis=1, tiled=True)
    picked = received[places]
    total = start_sum + jnp.einsum(
        "xmpt,xmts->xps", picked, blocks, preferred_element_type=jnp.float32
    )
    return total.astype(jnp.bfloat16)


def solution(mesh):
    placed = (
        P("wide", "narrow", None),
        P("wide", None),
        P("wide", "narrow"),
        P("wide", "narrow", None, None),
    )
    return jax.shard_map(
        functools.partial(on_device, mesh.shape["wide"]),
        mesh=mesh,
        in_specs=placed,
        out_specs=P("wide", "narrow", None),
        check_vma=False,
    )
```

time: 184 us -> 217 us (1.18)
  the two profiles are of different devices: /device:TPU:74 before, /device:TPU:465 now
where the time goes in v1:
time: 217 us
  Pallas kernels  176 us (81%)
  between operations  13.4 us (6%)
  blocking collectives  12.2 us (6%)
  local copies, waits for them, and re-layouts  8.4 us (4%)
  matrix products  5.41 us (2%)
    pallas_call x1, Pallas kernels, exchange(): pl.pallas_call(functools.partial(exchange_kernel, n_wide, cap), out_shape...  176 us
    all_gather x1, blocking collectives, on_device(): places = lax.all_gather(tile_positions, 'narrow', axis=1, tiled=True)  12.2 us
    dot_general x1, matrix products, on_device(): jnp.einsum('xmpt,xmts->xps', picked, blocks, preferred_element_type=jnp.f...  5.41 us
    gather x1, local copies, waits for them, and re-layouts, on_device(): picked = received[places]  5.22 us
  transfers between devices with their start and end apart: 1, of which 0 were waited for; matrix products, arithmetic and copies ran while one was open for 4% of the time, Pallas kernels for 81%

profile of v1, /device:TPU:465, one launch (start us, length us, event | category | flops | bytes accessed | tf_op | source)
XLA Modules:
  0.0 217.2 jit_solution(10775394007827901335)
XLA Ops:
  6.5 0.0 copy-start
  6.5 0.0 all-gather.3.cloned.1.call-start
  6.5 0.7 all-gather.3.cloned.1.call-update
  7.3 0.7 fusion.1
  7.9 0.0 copy-done
  7.9 3.0 %gather_fusion = bf16[128,128,128]{2,1,0:T(8,128)(2,1)} fusion(bf16[16,128,128]{2,1,0:T(8,128)(2,1)S(1)} %copy-done, s32[1024]{0:T(1024)S(1)} %pad_clamp_fusion.1), kind=kCustom, calls=%fused_computation | custom fusion | bytes 8389120 | tf_op jit(solution)/shard_map/gather | solution.py:78
  11.0 0.0 copy-start.1
  11.0 176.3 %shard_map.46 = bf16[128,128,128]{2,1,0:T(8,128)(2,1)} custom-call(bf16[128,128,128]{2,1,0:T(8,128)(2,1)} %gather_fusion), custom_call_target="tpu_custom_call" | custom-call | tf_op jit(solution)/shard_map/pallas_call | solution.py:62
  187.3 0.0 copy-done.1
  187.3 12.2 %all-gather = s32[8,2,8]{2,1,0:T(2,128)S(1)} all-gather(s32[1,2,8]{2,1,0:T(2,128)S(1)} %bitcast.20), channel_id=1, replica_groups=mesh['wide'=64,'narrow'=8] {'narrow'}, dimensions={0}, use_global_device_ids=true | all-gather | bytes 576 | tf_op jit(solution)/shard_map/all_gather | solution.py:82
  199.5 0.1 copy.6
  199.6 0.1 reshape.38
  199.7 5.2 %gather_fusion.1 = bf16[128,128,128]{2,1,0:T(8,128)(2,1)} fusion(bf16[128,128,128]{2,1,0:T(8,128)(2,1)} %shard_map.46, s32[1024]{0:T(1024)S(1)} %pad_clamp_fusion), kind=kCustom, calls=%fused_computation.1 | custom fusion | bytes 8389120 | tf_op jit(solution)/shard_map/gather | solution.py:83
  204.9 0.0 all-gather.3.cloned.1.call-done
  204.9 5.4 %fusion = bf16[8,128,128]{2,1,0:T(8,128)(2,1)} fusion(bf16[8,16,128,128]{3,2,1,0:T(8,128)(2,1)} %bitcast.18, bf16[8,16,128,128]{3,2,1,0:T(8,128)(2,1)} %all-gather.3.cloned.1.call-done), kind=kOutput, calls=%fused_computation.3 | convolution fusion | flops 537001984 | bytes 8650752 | tf_op jit(solution)/shard_map/xmpt,xmts->xps/dot_general | solution.py:84
  (3 shorter events, 0.0 us)
Async XLA Ops:
  6.5 1.4 copy-start
  6.5 198.4 %all-gather.3.cloned.1.call-start = ((), (), s32[]{:S(2)}) async-start(), calls=%async_computation | async-start | bytes 4718592 | tf_op jit(solution)/shard_map/all_gather | solution.py:81
  11.0 176.4 %copy-start.1 = (s32[8,2]{0,1:T(2,128)S(1)}, s32[8,2]{0,1:T(2,128)}, u32[]{:S(2)}) copy-start(s32[8,2]{0,1:T(2,128)} %param.6) | copy-start | bytes 196
Sparse Core Ops, SparseCore 0:
  9.5 37.2 all-gather.2

commit v2 on v0

v2 whole, which is shorter than its diff:
```python
import functools

import jax
import jax.numpy as jnp
from jax import lax
from jax.experimental import pallas as pl
from jax.experimental.pallas import tpu as pltpu
from jax.sharding import PartitionSpec as P


def ladder_kernel(n_k, places_ref, recv_ref, blk_ref, out_ref):
    x = pl.program_id(0)
    acc = jnp.zeros(out_ref.shape[1:], jnp.float32)
    for k in range(n_k):
        tile = recv_ref[places_ref[x * n_k + k]]
        acc = acc + jnp.dot(tile, blk_ref[0, k], preferred_element_type=jnp.float32)
    out_ref[0] = acc.astype(out_ref.dtype)


def ladder(places, received, blocks):
    n_x, n_k, t, s = blocks.shape
    n_recv, rows, _ = received.shape
    grid_spec = pltpu.PrefetchScalarGridSpec(
        num_scalar_prefetch=1,
        grid=(n_x,),
        in_specs=[
            pl.BlockSpec((n_recv, rows, t), lambda x, p: (0, 0, 0)),
            pl.BlockSpec((1, n_k, t, s), lambda x, p: (x, 0, 0, 0)),
        ],
        out_specs=pl.BlockSpec((1, rows, s), lambda x, p: (x, 0, 0)),
    )
    return pl.pallas_call(
        functools.partial(ladder_kernel, n_k),
        out_shape=jax.ShapeDtypeStruct((n_x, rows, s), jnp.bfloat16),
        grid_spec=grid_spec,
        cost_estimate=pl.CostEstimate(
            flops=2 * n_x * n_k * rows * t * s,
            transcendentals=0,
            bytes_accessed=2 * (received.size + blocks.size + n_x * rows * s),
        ),
    )(places.reshape(-1), received, blocks)


def on_device(amplitudes, send_list, tile_positions, integrals):
    outgoing = amplitudes[send_list[0]]
    received = lax.all_to_all(outgoing, "wide", split_axis=0, concat_axis=0, tiled=True)
    blocks = lax.all_gather(integrals, "narrow", axis=1, tiled=True)
    places = lax.all_gather(tile_positions, "narrow", axis=1, tiled=True)
    return ladder(places, received, blocks)


def solution(mesh):
    placed = (
        P("wide", "narrow", None),
        P("wide", None),
        P("wide", "narrow"),
        P("wide", "narrow", None, None),
    )
    return jax.shard_map(
        on_device, mesh=mesh, in_specs=placed, out_specs=P("wide", "narrow", None), check_vma=False
    )
```

time: 184 us -> 182 us (0.989)
  Pallas kernels: 0 us -> 8.73 us
  matrix products: 5.41 us -> 0 us
  local copies, waits for them, and re-layouts: 8.78 us -> 4.12 us
    all_to_all x1, waiting for transfers between devices: 130 us -> 98.9 us  [on_device(): lax.all_to_all(outgoing, 'wide', split_axis=0, concat_axis=0, tiled=True)]
    all_gather x1, waiting for transfers between devices: 0.01 us -> 30.1 us  [on_device(): blocks = lax.all_gather(integrals, 'narrow', axis=1, tiled=True)]
    pallas_call x0 -> x1, Pallas kernels: none -> 8.73 us  [ladder(): pl.pallas_call(functools.partial(ladder_kernel, n_k), out_shape=jax.Shape...]
    dot_general x1 -> x0, matrix products: 5.41 us -> none  [on_device(): jnp.einsum('xmpt,xmts->xps', picked, blocks, preferred_element_type=jnp.f...]
    gather x1 -> x0, local copies, waits for them, and re-layouts: 5.24 us -> none  [on_device(): picked = received[places]]
  transfers between devices with their start and end apart: 2 -> 2, of which waited for: 1 -> 2; matrix products, arithmetic and copies ran while one was open for 3% -> 0% of each run, Pallas kernels for 0% -> 0%
where the time goes in v2:
time: 182 us; the launch traced here: 181 us
  waiting for transfers between devices  130 us (71%)
  starting transfers between devices  16 us (9%)
  between operations  13.4 us (7%)
  Pallas kernels  8.73 us (5%)
  blocking collectives  8.68 us (5%)
  local copies, waits for them, and re-layouts  4.12 us (2%)
    all_to_all x1, waiting for transfers between devices, on_device(): lax.all_to_all(outgoing, 'wide', split_axis=0, concat_axis=0, tiled=True)  98.9 us
    all_gather x1, waiting for transfers between devices, on_device(): blocks = lax.all_gather(integrals, 'narrow', axis=1, tiled=True)  30.1 us
    all_to_all x1, starting transfers between devices, on_device(): lax.all_to_all(outgoing, 'wide', split_axis=0, concat_axis=0, tiled=True)  16 us
    pallas_call x1, Pallas kernels, ladder(): pl.pallas_call(functools.partial(ladder_kernel, n_k), out_shape=jax.Shape...  8.73 us
    all_gather x1, blocking collectives, on_device(): places = lax.all_gather(tile_positions, 'narrow', axis=1, tiled=True)  8.68 us
  transfers between devices with their start and end apart: 2, of which 2 were waited for; matrix products, arithmetic and copies ran while one was open for 0% of the time, Pallas kernels for 0%

profile of v2, /device:TPU:74, one launch (start us, length us, event | category | flops | bytes accessed | tf_op | source)
XLA Modules:
  0.0 181.4 jit_solution(17911359177458094198)
XLA Ops:
  6.5 0.0 copy-start
  6.5 0.7 fusion
  7.3 0.3 copy-done
  7.6 3.1 %gather_fusion = bf16[128,128,128]{2,1,0:T(8,128)(2,1)} fusion(bf16[16,128,128]{2,1,0:T(8,128)(2,1)S(1)} %copy-done, s32[1024]{0:T(1024)S(1)} %pad_clamp_fusion), kind=kCustom, calls=%fused_computation | custom fusion | bytes 8389120 | tf_op jit(solution)/shard_map/gather | solution.py:45
  10.6 0.0 copy-start.1
  10.6 16.0 %all-to-all-start = ((bf16[128,128,128]{2,1,0:T(8,128)(2,1)}), bf16[128,128,128]{2,1,0:T(8,128)(2,1)}, u32[]{:S(2)}, u32[]{:S(2)}) async-start(bf16[128,128,128]{2,1,0:T(8,128)(2,1)} %gather_fusion), calls=%async_computation | async-start | bytes 8388608 | tf_op jit(solution)/shard_map/all_to_all | solution.py:46
  26.7 0.0 all-gather.3.cloned.1.call-start
  26.7 0.7 all-gather.3.cloned.1.call-update
  27.4 0.0 copy-done.1
  27.4 8.7 %all-gather = s32[8,2,8]{2,1,0:T(2,128)S(1)} all-gather(s32[1,2,8]{2,1,0:T(2,128)S(1)} %bitcast.11), channel_id=1, replica_groups=mesh['wide'=64,'narrow'=8] {'narrow'}, dimensions={0}, use_global_device_ids=true | all-gather | bytes 576 | tf_op jit(solution)/shard_map/all_gather | solution.py:48
  36.1 0.1 copy.6
  36.1 0.7 reshape.31.places_ref
  36.8 30.1 %all-gather.3.cloned.1.call-done.blk_ref = bf16[8,16,128,128]{3,2,1,0:T(8,128)(2,1)} async-done(((bf16[8,2,128,128]{3,2,1,0:T(8,128)(2,1)}), bf16[8,16,128,128]{3,2,1,0:T(8,128)(2,1)}) %all-gather.3.cloned.1.call-update) | async-done | bytes 4194320 | tf_op jit(solution)/shard_map/all_gather | solution.py:47
  66.9 98.9 %all-to-all-done.recv_ref = bf16[128,128,128]{2,1,0:T(8,128)(2,1)} async-done(((bf16[128,128,128]{2,1,0:T(8,128)(2,1)}), bf16[128,128,128]{2,1,0:T(8,128)(2,1)}, u32[]{:S(2)}, u32[]{:S(2)}) %all-to-all-start) | async-done | bytes 4194336 | tf_op jit(solution)/shard_map/all_to_all | solution.py:46
  165.8 8.7 %shard_map.46 = bf16[8,128,128]{2,1,0:T(8,128)(2,1)} custom-call(s32[128]{0:T(128)} %reshape.31.places_ref, bf16[128,128,128]{2,1,0:T(8,128)(2,1)} %all-to-all-done.recv_ref, bf16[8,16,128,128]{3,2,1,0:T(8,128)(2,1)} %all-gather.3.cloned.1.call-done.blk_ref), custom_call_target="tpu_custom_call" | custom-call | flops 536870912 | bytes 8650752 | tf_op jit(solution)/shard_map/pallas_call | solution.py:32
  (1 shorter events, 0.0 us)
Async XLA Ops:
  6.5 1.1 copy-start
  10.6 16.7 %copy-start.1 = (s32[8,2]{0,1:T(2,128)S(1)}, s32[8,2]{0,1:T(2,128)}, u32[]{:S(2)}) copy-start(s32[8,2]{0,1:T(2,128)} %param.6) | copy-start | bytes 196
  10.6 155.2 %all-to-all-start = ((bf16[128,128,128]{2,1,0:T(8,128)(2,1)}), bf16[128,128,128]{2,1,0:T(8,128)(2,1)}, u32[]{:S(2)}, u32[]{:S(2)}) async-start(bf16[128,128,128]{2,1,0:T(8,128)(2,1)} %gather_fusion), calls=%async_computation | async-start | bytes 8388608 | tf_op jit(solution)/shard_map/all_to_all | solution.py:46
  26.7 40.3 %all-gather.3.cloned.1.call-start = ((), (), s32[]{:S(2)}) async-start(), calls=%async_computation.1 | async-start | bytes 4718592 | tf_op jit(solution)/shard_map/all_gather | solution.py:47
Sparse Core Ops, SparseCore 0:
  29.6 37.2 all-gather.2

commit v3 on v2

v3 whole, which is shorter than its diff:
```python
import functools

import jax
import jax.numpy as jnp
from jax import lax
from jax.experimental import pallas as pl
from jax.experimental.pallas import tpu as pltpu
from jax.sharding import PartitionSpec as P

MESH = pl.DeviceIdType.MESH


def gather_kernel(n_nar, src_ref, dst_ref, send_sem, recv_sem, local_sem):
    me = lax.axis_index("narrow")
    w = lax.axis_index("wide")

    barrier = pltpu.get_barrier_semaphore()
    for i in range(1, n_nar):
        peer = lax.rem(me + i, n_nar)
        pl.semaphore_signal(barrier, 1, device_id=(w, peer), device_id_type=MESH)
    pl.semaphore_wait(barrier, n_nar - 1)

    local = pltpu.make_async_copy(src_ref, dst_ref.at[me], local_sem)
    local.start()

    def remote(peer, slot):
        return pltpu.make_async_remote_copy(
            src_ref=src_ref,
            dst_ref=dst_ref.at[slot],
            send_sem=send_sem.at[peer],
            recv_sem=recv_sem.at[slot],
            device_id=(w, peer),
            device_id_type=MESH,
        )

    for i in range(1, n_nar):
        remote(lax.rem(me + i, n_nar), me).start()
    for i in range(1, n_nar):
        remote(lax.rem(me + i, n_nar), me).wait_send()
        owner = lax.rem(me + n_nar - i, n_nar)
        remote(owner, owner).wait_recv()
    local.wait()


def gather_integrals(integrals, n_nar):
    return pl.pallas_call(
        functools.partial(gather_kernel, n_nar),
        out_shape=jax.ShapeDtypeStruct((n_nar,) + integrals.shape, integrals.dtype),
        in_specs=[pl.BlockSpec(memory_space=pl.ANY)],
        out_specs=pl.BlockSpec(memory_space=pl.ANY),
        scratch_shapes=[
            pltpu.SemaphoreType.DMA((n_nar,)),
            pltpu.SemaphoreType.DMA((n_nar,)),
            pltpu.SemaphoreType.DMA,
        ],
        compiler_params=pltpu.CompilerParams(collective_id=0, has_side_effects=True),
        cost_estimate=pl.CostEstimate(
            flops=0, transcendentals=0, bytes_accessed=2 * n_nar * integrals.size * 2
        ),
    )(integrals)


def ladder_kernel(n_k, per, places_ref, recv_ref, blk_ref, out_ref):
    x = pl.program_id(0)
    tiles = [recv_ref[places_ref[x * n_k + k]] for k in range(n_k)]
    lhs = jnp.concatenate(tiles, axis=1)
    rhs = blk_ref[...].reshape(n_k * blk_ref.shape[-2], blk_ref.shape[-1])
    out_ref[0] = jnp.dot(lhs, rhs, preferred_element_type=jnp.float32).astype(out_ref.dtype)


def ladder(places, received, blocks):
    n_nar, n_x, per, t, s = blocks.shape
    n_k = n_nar * per
    n_recv, rows, _ = received.shape
    grid_spec = pltpu.PrefetchScalarGridSpec(
        num_scalar_prefetch=1,
        grid=(n_x,),
        in_specs=[
            pl.BlockSpec((n_recv, rows, t), lambda x, p: (0, 0, 0)),
            pl.BlockSpec((n_nar, 1, per, t, s), lambda x, p: (0, x, 0, 0, 0)),
        ],
        out_specs=pl.BlockSpec((1, rows, s), lambda x, p: (x, 0, 0)),
    )
    return pl.pallas_call(
        functools.partial(ladder_kernel, n_k, per),
        out_shape=jax.ShapeDtypeStruct((n_x, rows, s), jnp.bfloat16),
        grid_spec=grid_spec,
        cost_estimate=pl.CostEstimate(
            flops=2 * n_x * n_k * rows * t * s,
            transcendentals=0,
            bytes_accessed=2 * (received.size + blocks.size + n_x * rows * s),
        ),
    )(places.reshape(-1), received, blocks)


def on_device(n_nar, amplitudes, send_list, tile_positions, integrals):
    outgoing = amplitudes[send_list[0]]
    received = lax.all_to_all(outgoing, "wide", split_axis=0, concat_axis=0, tiled=True)
    blocks = gather_integrals(integrals, n_nar)
    places = lax.all_gather(tile_positions, "narrow", axis=1, tiled=True)
    return ladder(places, received, blocks)


def solution(mesh):
    placed = (
        P("wide", "narrow", None),
        P("wide", None),
        P("wide", "narrow"),
        P("wide", "narrow", None, None),
    )
    return jax.shard_map(
        functools.partial(on_device, mesh.shape["narrow"]),
        mesh=mesh,
        in_specs=placed,
        out_specs=P("wide", "narrow", None),
        check_vma=False,
    )
```

time: 182 us -> 168 us (0.923)
  the two profiles are of different devices: /device:TPU:74 before, /device:TPU:76 now
where the time goes in v3:
time: 168 us
  waiting for transfers between devices  80.6 us (48%)
  Pallas kernels  58.2 us (35%)
  starting transfers between devices  16 us (10%)
  blocking collectives  8.39 us (5%)
  local copies, waits for them, and re-layouts  4.08 us (2%)
    all_to_all x1, waiting for transfers between devices, on_device(): lax.all_to_all(outgoing, 'wide', split_axis=0, concat_axis=0, tiled=True)  80.6 us
    pallas_call x1, Pallas kernels, gather_integrals(): pl.pallas_call(functools.partial(gather_kernel, n_nar), out_shape=jax.Sha...  49.5 us
    all_to_all x1, starting transfers between devices, on_device(): lax.all_to_all(outgoing, 'wide', split_axis=0, concat_axis=0, tiled=True)  16 us
    pallas_call x1, Pallas kernels, ladder(): pl.pallas_call(functools.partial(ladder_kernel, n_k, per), out_shape=jax....  8.71 us
    all_gather x1, blocking collectives, on_device(): places = lax.all_gather(tile_positions, 'narrow', axis=1, tiled=True)  8.39 us
  transfers between devices with their start and end apart: 1, of which 1 were waited for; matrix products, arithmetic and copies ran while one was open for 0% of the time, Pallas kernels for 29%

profile of v3, /device:TPU:76, one launch (start us, length us, event | category | flops | bytes accessed | tf_op | source)
XLA Modules:
  0.0 168.0 jit_solution(4418845585755647170)
XLA Ops:
  0.0 0.0 copy-start
  0.0 0.7 fusion
  0.7 0.3 copy-done
  1.1 3.1 %gather_fusion = bf16[128,128,128]{2,1,0:T(8,128)(2,1)} fusion(bf16[16,128,128]{2,1,0:T(8,128)(2,1)S(1)} %copy-done, s32[1024]{0:T(1024)S(1)} %pad_clamp_fusion), kind=kCustom, calls=%fused_computation | custom fusion | bytes 8389120 | tf_op jit(solution)/shard_map/gather | solution.py:97
  4.1 0.0 copy-start.1
  4.1 16.0 %all-to-all-start = ((bf16[128,128,128]{2,1,0:T(8,128)(2,1)}), bf16[128,128,128]{2,1,0:T(8,128)(2,1)}, u32[]{:S(2)}, u32[]{:S(2)}) async-start(bf16[128,128,128]{2,1,0:T(8,128)(2,1)} %gather_fusion), calls=%async_computation | async-start | bytes 8388608 | tf_op jit(solution)/shard_map/all_to_all | solution.py:98
  20.1 0.0 copy-done.1
  20.1 8.4 %all-gather = s32[8,2,8]{2,1,0:T(2,128)S(1)} all-gather(s32[1,2,8]{2,1,0:T(2,128)S(1)} %bitcast.11), channel_id=1, replica_groups=mesh['wide'=64,'narrow'=8] {'narrow'}, dimensions={0}, use_global_device_ids=true | all-gather | bytes 576 | tf_op jit(solution)/shard_map/all_gather | solution.py:100
  28.5 0.1 copy.6
  28.6 0.6 reshape.31.places_ref
  29.2 49.5 %shard_map.46.blk_ref = bf16[8,8,2,128,128]{4,3,2,1,0:T(8,128)(2,1)} custom-call(bf16[8,2,128,128]{3,2,1,0:T(8,128)(2,1)} %src_ref.1), custom_call_target="tpu_custom_call" | custom-call | bytes 8388608 | tf_op jit(solution)/shard_map/pallas_call | solution.py:46
  78.7 80.6 %all-to-all-done.recv_ref = bf16[128,128,128]{2,1,0:T(8,128)(2,1)} async-done(((bf16[128,128,128]{2,1,0:T(8,128)(2,1)}), bf16[128,128,128]{2,1,0:T(8,128)(2,1)}, u32[]{:S(2)}, u32[]{:S(2)}) %all-to-all-start) | async-done | bytes 4194336 | tf_op jit(solution)/shard_map/all_to_all | solution.py:98
  159.3 8.7 %shard_map.47 = bf16[8,128,128]{2,1,0:T(8,128)(2,1)} custom-call(s32[128]{0:T(128)} %reshape.31.places_ref, bf16[128,128,128]{2,1,0:T(8,128)(2,1)} %all-to-all-done.recv_ref, bf16[8,8,2,128,128]{4,3,2,1,0:T(8,128)(2,1)} %shard_map.46.blk_ref), custom_call_target="tpu_custom_call" | custom-call | flops 536870912 | bytes 8650752 | tf_op jit(solution)/shard_map/pallas_call | solution.py:84
  (1 shorter events, 0.0 us)
Async XLA Ops:
  0.0 1.1 copy-start
  4.1 16.0 %copy-start.1 = (s32[8,2]{0,1:T(2,128)S(1)}, s32[8,2]{0,1:T(2,128)}, u32[]{:S(2)}) copy-start(s32[8,2]{0,1:T(2,128)} %param.6) | copy-start | bytes 196
  4.1 155.2 %all-to-all-start = ((bf16[128,128,128]{2,1,0:T(8,128)(2,1)}), bf16[128,128,128]{2,1,0:T(8,128)(2,1)}, u32[]{:S(2)}, u32[]{:S(2)}) async-start(bf16[128,128,128]{2,1,0:T(8,128)(2,1)} %gather_fusion), calls=%async_computation | async-start | bytes 8388608 | tf_op jit(solution)/shard_map/all_to_all | solution.py:98

commit v4 on v3

--- a/solution.py
+++ b/solution.py
@@ -60,35 +60,50 @@
     )(integrals)
 
 
-def ladder_kernel(n_k, per, places_ref, recv_ref, blk_ref, out_ref):
-    x = pl.program_id(0)
-    tiles = [recv_ref[places_ref[x * n_k + k]] for k in range(n_k)]
-    lhs = jnp.concatenate(tiles, axis=1)
-    rhs = blk_ref[...].reshape(n_k * blk_ref.shape[-2], blk_ref.shape[-1])
-    out_ref[0] = jnp.dot(lhs, rhs, preferred_element_type=jnp.float32).astype(out_ref.dtype)
+def ladder_kernel(n_x, n_k, places_ref, recv_hbm, blk_hbm, out_ref, tiles, blks, sems):
+    def copies(x, slot):
+        picked = [
+            pltpu.make_async_copy(recv_hbm.at[places_ref[x * n_k + k]], tiles.at[slot, k], sems.at[slot, k])
+            for k in range(n_k)
+        ]
+        return picked + [pltpu.make_async_copy(blk_hbm.at[:, x], blks.at[slot], sems.at[slot, n_k])]
+
+    for c in copies(0, 0):
+        c.start()
+    for x in range(n_x):
+        slot = x % 2
+        if x + 1 < n_x:
+            for c in copies(x + 1, 1 - slot):
+                c.start()
+        for c in copies(x, slot):
+            c.wait()
+        lhs = jnp.concatenate([tiles[slot, k] for k in range(n_k)], axis=1)
+        rhs = blks[slot].reshape(n_k * blks.shape[-2], blks.shape[-1])
+        out_ref[x] = jnp.dot(lhs, rhs, preferred_element_type=jnp.float32).astype(out_ref.dtype)
 
 
 def ladder(places, received, blocks):
     n_nar, n_x, per, t, s = blocks.shape
     n_k = n_nar * per
     n_recv, rows, _ = received.shape
-    grid_spec = pltpu.PrefetchScalarGridSpec(
-        num_scalar_prefetch=1,
-        grid=(n_x,),
+    return pl.pallas_call(
+        functools.partial(ladder_kernel, n_x, n_k),
+        out_shape=jax.ShapeDtypeStruct((n_x, rows, s), jnp.bfloat16),
         in_specs=[
-            pl.BlockSpec((n_recv, rows, t), lambda x, p: (0, 0, 0)),
-            pl.BlockSpec((n_nar, 1, per, t, s), lambda x, p: (0, x, 0, 0, 0)),
+            pl.BlockSpec(memory_space=pltpu.SMEM),
+            pl.BlockSpec(memory_space=pl.ANY),
+            pl.BlockSpec(memory_space=pl.ANY),
         ],
-        out_specs=pl.BlockSpec((1, rows, s), lambda x, p: (x, 0, 0)),
-    )
-    return pl.pallas_call(
-        functools.partial(ladder_kernel, n_k, per),
-        out_shape=jax.ShapeDtypeStruct((n_x, rows, s), jnp.bfloat16),
-        grid_spec=grid_spec,
+        out_specs=pl.BlockSpec(memory_space=pltpu.VMEM),
+        scratch_shapes=[
+            pltpu.VMEM((2, n_k, rows, t), received.dtype),
+            pltpu.VMEM((2, n_nar, per, t, s), blocks.dtype),
+            pltpu.SemaphoreType.DMA((2, n_k + 1)),
+        ],
         cost_estimate=pl.CostEstimate(
             flops=2 * n_x * n_k * rows * t * s,
             transcendentals=0,
-            bytes_accessed=2 * (received.size + blocks.size + n_x * rows * s),
+            bytes_accessed=2 * (2 * blocks.size + n_x * rows * s),
         ),
     )(places.reshape(-1), received, blocks)
 

time: 168 us -> 168 us (level)
  transfers between devices with their start and end apart: 1 -> 1, of which waited for: 1 -> 1; matrix products, arithmetic and copies ran while one was open for 0% -> 0% of each run, Pallas kernels for 29% -> 30%
where the time goes in v4:
time: 168 us; the launch traced here: 167 us
  waiting for transfers between devices  80.6 us (48%)
  Pallas kernels  57.6 us (34%)
  starting transfers between devices  16 us (10%)
  blocking collectives  8.39 us (5%)
  local copies, waits for them, and re-layouts  4.08 us (2%)
    all_to_all x1, waiting for transfers between devices, on_device(): lax.all_to_all(outgoing, 'wide', split_axis=0, concat_axis=0, tiled=True)  80.6 us
    pallas_call x1, Pallas kernels, gather_integrals(): pl.pallas_call(functools.partial(gather_kernel, n_nar), out_shape=jax.Sha...  49.5 us
    all_to_all x1, starting transfers between devices, on_device(): lax.all_to_all(outgoing, 'wide', split_axis=0, concat_axis=0, tiled=True)  16 us
    all_gather x1, blocking collectives, on_device(): places = lax.all_gather(tile_positions, 'narrow', axis=1, tiled=True)  8.39 us
    pallas_call x1, Pallas kernels, ladder(): pl.pallas_call(functools.partial(ladder_kernel, n_x, n_k), out_shape=jax....  8.08 us
  transfers between devices with their start and end apart: 1, of which 1 were waited for; matrix products, arithmetic and copies ran while one was open for 0% of the time, Pallas kernels for 30%

profile of v4, /device:TPU:76, one launch (start us, length us, event | category | flops | bytes accessed | tf_op | source)
XLA Modules:
  0.0 167.4 jit_solution(15909569281023419302)
XLA Ops:
  0.0 0.0 copy-start
  0.0 0.7 fusion
  0.7 0.3 copy-done
  1.1 3.1 %gather_fusion = bf16[128,128,128]{2,1,0:T(8,128)(2,1)} fusion(bf16[16,128,128]{2,1,0:T(8,128)(2,1)S(1)} %copy-done, s32[1024]{0:T(1024)S(1)} %pad_clamp_fusion), kind=kCustom, calls=%fused_computation | custom fusion | bytes 8389120 | tf_op jit(solution)/shard_map/gather | solution.py:112
  4.1 0.0 copy-start.1
  4.1 16.0 %all-to-all-start = ((bf16[128,128,128]{2,1,0:T(8,128)(2,1)}), bf16[128,128,128]{2,1,0:T(8,128)(2,1)}, u32[]{:S(2)}, u32[]{:S(2)}) async-start(bf16[128,128,128]{2,1,0:T(8,128)(2,1)} %gather_fusion), calls=%async_computation | async-start | bytes 8388608 | tf_op jit(solution)/shard_map/all_to_all | solution.py:113
  20.1 0.0 copy-done.1
  20.1 8.4 %all-gather = s32[8,2,8]{2,1,0:T(2,128)S(1)} all-gather(s32[1,2,8]{2,1,0:T(2,128)S(1)} %bitcast.11), channel_id=1, replica_groups=mesh['wide'=64,'narrow'=8] {'narrow'}, dimensions={0}, use_global_device_ids=true | all-gather | bytes 576 | tf_op jit(solution)/shard_map/all_gather | solution.py:115
  28.5 0.1 copy.6
  28.6 0.6 reshape.31.places_ref
  29.2 49.5 %shard_map.46.blk_hbm = bf16[8,8,2,128,128]{4,3,2,1,0:T(8,128)(2,1)} custom-call(bf16[8,2,128,128]{3,2,1,0:T(8,128)(2,1)} %src_ref.1), custom_call_target="tpu_custom_call" | custom-call | bytes 8388608 | tf_op jit(solution)/shard_map/pallas_call | solution.py:46
  78.7 80.6 %all-to-all-done.recv_hbm = bf16[128,128,128]{2,1,0:T(8,128)(2,1)} async-done(((bf16[128,128,128]{2,1,0:T(8,128)(2,1)}), bf16[128,128,128]{2,1,0:T(8,128)(2,1)}, u32[]{:S(2)}, u32[]{:S(2)}) %all-to-all-start) | async-done | bytes 4194336 | tf_op jit(solution)/shard_map/all_to_all | solution.py:113
  159.3 8.1 %shard_map.47 = bf16[8,128,128]{2,1,0:T(8,128)(2,1)} custom-call(s32[128]{0:T(128)} %reshape.31.places_ref, bf16[128,128,128]{2,1,0:T(8,128)(2,1)} %all-to-all-done.recv_hbm, bf16[8,8,2,128,128]{4,3,2,1,0:T(8,128)(2,1)} %shard_map.46.blk_hbm), custom_call_target="tpu_custom_call" | custom-call | flops 536870912 | bytes 8650752 | tf_op jit(solution)/shard_map/pallas_call | solution.py:89
  (1 shorter events, 0.0 us)
Async XLA Ops:
  0.0 1.1 copy-start
  4.1 16.0 %copy-start.1 = (s32[8,2]{0,1:T(2,128)S(1)}, s32[8,2]{0,1:T(2,128)}, u32[]{:S(2)}) copy-start(s32[8,2]{0,1:T(2,128)} %param.6) | copy-start | bytes 196
  4.1 155.2 %all-to-all-start = ((bf16[128,128,128]{2,1,0:T(8,128)(2,1)}), bf16[128,128,128]{2,1,0:T(8,128)(2,1)}, u32[]{:S(2)}, u32[]{:S(2)}) async-start(bf16[128,128,128]{2,1,0:T(8,128)(2,1)} %gather_fusion), calls=%async_computation | async-start | bytes 8388608 | tf_op jit(solution)/shard_map/all_to_all | solution.py:113

commit v5 on v4

--- a/solution.py
+++ b/solution.py
@@ -108,8 +108,28 @@
     )(places.reshape(-1), received, blocks)
 
 
+def pick_kernel(n_out, sel_ref, amp_ref, out_hbm, sems):
+    copies = [pltpu.make_async_copy(amp_ref.at[sel_ref[j]], out_hbm.at[j], sems.at[j]) for j in range(n_out)]
+    for c in copies:
+        c.start()
+    for c in copies:
+        c.wait()
+
+
+def pick_outgoing(amplitudes, selection):
+    n_out = selection.shape[0]
+    return pl.pallas_call(
+        functools.partial(pick_kernel, n_out),
+        out_shape=jax.ShapeDtypeStruct((n_out,) + amplitudes.shape[1:], amplitudes.dtype),
+        in_specs=[pl.BlockSpec(memory_space=pltpu.SMEM), pl.BlockSpec(memory_space=pltpu.VMEM)],
+        out_specs=pl.BlockSpec(memory_space=pl.ANY),
+        scratch_shapes=[pltpu.SemaphoreType.DMA((n_out,))],
+        cost_estimate=pl.CostEstimate(flops=0, transcendentals=0, bytes_accessed=4 * n_out * amplitudes[0].size),
+    )(selection, amplitudes)
+
+
 def on_device(n_nar, amplitudes, send_list, tile_positions, integrals):
-    outgoing = amplitudes[send_list[0]]
+    outgoing = pick_outgoing(amplitudes, send_list[0])
     received = lax.all_to_all(outgoing, "wide", split_axis=0, concat_axis=0, tiled=True)
     blocks = gather_integrals(integrals, n_nar)
     places = lax.all_gather(tile_positions, "narrow", axis=1, tiled=True)

time: 168 us -> 168 us (level)
  Pallas kernels: 57.6 us -> 61.8 us
  local copies, waits for them, and re-layouts: 4.08 us -> 0.74 us
    pallas_call x0 -> x1, Pallas kernels: none -> 4.17 us  [pick_outgoing(): pl.pallas_call(functools.partial(pick_kernel, n_out), out_shape=jax.Shape...]
    gather x1 -> x0, local copies, waits for them, and re-layouts: 3.05 us -> none  [on_device(): outgoing = amplitudes[send_list[0]]]
where the time goes in v5:
time: 168 us; the launch traced here: 167 us
  waiting for transfers between devices  80.5 us (48%)
  Pallas kernels  61.8 us (37%)
  starting transfers between devices  15.9 us (9%)
  blocking collectives  8.39 us (5%)
    all_to_all x1, waiting for transfers between devices, on_device(): lax.all_to_all(outgoing, 'wide', split_axis=0, concat_axis=0, tiled=True)  80.5 us
    pallas_call x1, Pallas kernels, gather_integrals(): pl.pallas_call(functools.partial(gather_kernel, n_nar), out_shape=jax.Sha...  49.5 us
    all_to_all x1, starting transfers between devices, on_device(): lax.all_to_all(outgoing, 'wide', split_axis=0, concat_axis=0, tiled=True)  15.9 us
    all_gather x1, blocking collectives, on_device(): places = lax.all_gather(tile_positions, 'narrow', axis=1, tiled=True)  8.39 us
    pallas_call x1, Pallas kernels, ladder(): pl.pallas_call(functools.partial(ladder_kernel, n_x, n_k), out_shape=jax....  8.17 us
    pallas_call x1, Pallas kernels, pick_outgoing(): pl.pallas_call(functools.partial(pick_kernel, n_out), out_shape=jax.Shape...  4.17 us
  transfers between devices with their start and end apart: 1, of which 1 were waited for; matrix products, arithmetic and copies ran while one was open for 0% of the time, Pallas kernels for 30%

profile of v5, /device:TPU:76, one launch (start us, length us, event | category | flops | bytes accessed | tf_op | source)
XLA Modules:
  0.0 167.4 jit_solution(8667962042107072433)
XLA Ops:
  0.0 4.2 %shard_map.46 = bf16[128,128,128]{2,1,0:T(8,128)(2,1)} custom-call(s32[128]{0:T(128)} %bitcast.9, bf16[16,128,128]{2,1,0:T(8,128)(2,1)} %amp_ref.1), custom_call_target="tpu_custom_call" | custom-call | bytes 8388608 | tf_op jit(solution)/shard_map/pallas_call | solution.py:121
  4.2 0.0 copy-start
  4.2 15.9 %all-to-all-start = ((bf16[128,128,128]{2,1,0:T(8,128)(2,1)}), bf16[128,128,128]{2,1,0:T(8,128)(2,1)}, u32[]{:S(2)}, u32[]{:S(2)}) async-start(bf16[128,128,128]{2,1,0:T(8,128)(2,1)} %shard_map.46), calls=%async_computation | async-start | bytes 8388608 | tf_op jit(solution)/shard_map/all_to_all | solution.py:133
  20.1 0.0 copy-done
  20.1 8.4 %all-gather = s32[8,2,8]{2,1,0:T(2,128)S(1)} all-gather(s32[1,2,8]{2,1,0:T(2,128)S(1)} %bitcast.8), channel_id=1, replica_groups=mesh['wide'=64,'narrow'=8] {'narrow'}, dimensions={0}, use_global_device_ids=true | all-gather | bytes 576 | tf_op jit(solution)/shard_map/all_gather | solution.py:135
  28.5 0.1 copy.6
  28.5 0.7 reshape.3.places_ref
  29.2 49.5 %shard_map.47.blk_hbm = bf16[8,8,2,128,128]{4,3,2,1,0:T(8,128)(2,1)} custom-call(bf16[8,2,128,128]{3,2,1,0:T(8,128)(2,1)} %src_ref.1), custom_call_target="tpu_custom_call" | custom-call | bytes 8388608 | tf_op jit(solution)/shard_map/pallas_call | solution.py:46
  78.7 80.5 %all-to-all-done.recv_hbm = bf16[128,128,128]{2,1,0:T(8,128)(2,1)} async-done(((bf16[128,128,128]{2,1,0:T(8,128)(2,1)}), bf16[128,128,128]{2,1,0:T(8,128)(2,1)}, u32[]{:S(2)}, u32[]{:S(2)}) %all-to-all-start) | async-done | bytes 4194336 | tf_op jit(solution)/shard_map/all_to_all | solution.py:133
  159.2 8.2 %shard_map.48 = bf16[8,128,128]{2,1,0:T(8,128)(2,1)} custom-call(s32[128]{0:T(128)} %reshape.3.places_ref, bf16[128,128,128]{2,1,0:T(8,128)(2,1)} %all-to-all-done.recv_hbm, bf16[8,8,2,128,128]{4,3,2,1,0:T(8,128)(2,1)} %shard_map.47.blk_hbm), custom_call_target="tpu_custom_call" | custom-call | flops 536870912 | bytes 8650752 | tf_op jit(solution)/shard_map/pallas_call | solution.py:89
Async XLA Ops:
  4.2 15.9 %copy-start = (s32[8,2]{0,1:T(2,128)S(1)}, s32[8,2]{0,1:T(2,128)}, u32[]{:S(2)}) copy-start(s32[8,2]{0,1:T(2,128)} %param.6) | copy-start | bytes 196
  4.2 155.0 %all-to-all-start = ((bf16[128,128,128]{2,1,0:T(8,128)(2,1)}), bf16[128,128,128]{2,1,0:T(8,128)(2,1)}, u32[]{:S(2)}, u32[]{:S(2)}) async-start(bf16[128,128,128]{2,1,0:T(8,128)(2,1)} %shard_map.46), calls=%async_computation | async-start | bytes 8388608 | tf_op jit(solution)/shard_map/all_to_all | solution.py:133

commit v6 on v5

--- a/solution.py
+++ b/solution.py
@@ -8,6 +8,7 @@
 from jax.sharding import PartitionSpec as P
 
 MESH = pl.DeviceIdType.MESH
+CUT = 64
 
 
 def gather_kernel(n_nar, src_ref, dst_ref, send_sem, recv_sem, local_sem):
@@ -60,13 +61,18 @@
     )(integrals)
 
 
-def ladder_kernel(n_x, n_k, places_ref, recv_hbm, blk_hbm, out_ref, tiles, blks, sems):
+def ladder_kernel(n_x, n_k, places_ref, head_hbm, tail_hbm, blk_hbm, out_ref, tiles, blks, sems):
     def copies(x, slot):
-        picked = [
-            pltpu.make_async_copy(recv_hbm.at[places_ref[x * n_k + k]], tiles.at[slot, k], sems.at[slot, k])
-            for k in range(n_k)
-        ]
-        return picked + [pltpu.make_async_copy(blk_hbm.at[:, x], blks.at[slot], sems.at[slot, n_k])]
+        cut = head_hbm.shape[1]
+        picked = []
+        for k in range(n_k):
+            p = places_ref[x * n_k + k]
+            dst = tiles.at[slot, k]
+            picked.append(pltpu.make_async_copy(head_hbm.at[p], dst.at[pl.ds(0, cut)], sems.at[slot, 0, k]))
+            picked.append(
+                pltpu.make_async_copy(tail_hbm.at[p], dst.at[pl.ds(cut, dst.shape[0] - cut)], sems.at[slot, 1, k])
+            )
+        return picked + [pltpu.make_async_copy(blk_hbm.at[:, x], blks.at[slot], sems.at[slot, 2, 0])]
 
     for c in copies(0, 0):
         c.start()
@@ -82,10 +88,10 @@
         out_ref[x] = jnp.dot(lhs, rhs, preferred_element_type=jnp.float32).astype(out_ref.dtype)
 
 
-def ladder(places, received, blocks):
+def ladder(places, head, tail, blocks):
     n_nar, n_x, per, t, s = blocks.shape
     n_k = n_nar * per
-    n_recv, rows, _ = received.shape
+    rows = head.shape[1] + tail.shape[1]
     return pl.pallas_call(
         functools.partial(ladder_kernel, n_x, n_k),
         out_shape=jax.ShapeDtypeStruct((n_x, rows, s), jnp.bfloat16),
@@ -93,47 +99,56 @@
             pl.BlockSpec(memory_space=pltpu.SMEM),
             pl.BlockSpec(memory_space=pl.ANY),
             pl.BlockSpec(memory_space=pl.ANY),
+            pl.BlockSpec(memory_space=pl.ANY),
         ],
         out_specs=pl.BlockSpec(memory_space=pltpu.VMEM),
         scratch_shapes=[
-            pltpu.VMEM((2, n_k, rows, t), received.dtype),
+            pltpu.VMEM((2, n_k, rows, t), head.dtype),
             pltpu.VMEM((2, n_nar, per, t, s), blocks.dtype),
-            pltpu.SemaphoreType.DMA((2, n_k + 1)),
+            pltpu.SemaphoreType.DMA((2, 3, n_k)),
         ],
         cost_estimate=pl.CostEstimate(
             flops=2 * n_x * n_k * rows * t * s,
             transcendentals=0,
             bytes_accessed=2 * (2 * blocks.size + n_x * rows * s),
         ),
-    )(places.reshape(-1), received, blocks)
+    )(places.reshape(-1), head, tail, blocks)
 
 
-def pick_kernel(n_out, sel_ref, amp_ref, out_hbm, sems):
-    copies = [pltpu.make_async_copy(amp_ref.at[sel_ref[j]], out_hbm.at[j], sems.at[j]) for j in range(n_out)]
+def pick_kernel(n_out, cut, sel_ref, amp_ref, head_hbm, tail_hbm, sems):
+    copies = []
+    for j in range(n_out):
+        src = amp_ref.at[sel_ref[j]]
+        copies.append(pltpu.make_async_copy(src.at[pl.ds(0, cut)], head_hbm.at[j], sems.at[0, j]))
+        copies.append(pltpu.make_async_copy(src.at[pl.ds(cut, src.shape[0] - cut)], tail_hbm.at[j], sems.at[1, j]))
     for c in copies:
         c.start()
     for c in copies:
         c.wait()
 
 
-def pick_outgoing(amplitudes, selection):
-    n_out = selection.shape[0]
+def pick_outgoing(amplitudes, selection, cut):
+    n_out, (rows, t) = selection.shape[0], amplitudes.shape[1:]
     return pl.pallas_call(
-        functools.partial(pick_kernel, n_out),
-        out_shape=jax.ShapeDtypeStruct((n_out,) + amplitudes.shape[1:], amplitudes.dtype),
+        functools.partial(pick_kernel, n_out, cut),
+        out_shape=(
+            jax.ShapeDtypeStruct((n_out, cut, t), amplitudes.dtype),
+            jax.ShapeDtypeStruct((n_out, rows - cut, t), amplitudes.dtype),
+        ),
         in_specs=[pl.BlockSpec(memory_space=pltpu.SMEM), pl.BlockSpec(memory_space=pltpu.VMEM)],
-        out_specs=pl.BlockSpec(memory_space=pl.ANY),
-        scratch_shapes=[pltpu.SemaphoreType.DMA((n_out,))],
+        out_specs=(pl.BlockSpec(memory_space=pl.ANY), pl.BlockSpec(memory_space=pl.ANY)),
+        scratch_shapes=[pltpu.SemaphoreType.DMA((2, n_out))],
         cost_estimate=pl.CostEstimate(flops=0, transcendentals=0, bytes_accessed=4 * n_out * amplitudes[0].size),
     )(selection, amplitudes)
 
 
 def on_device(n_nar, amplitudes, send_list, tile_positions, integrals):
-    outgoing = pick_outgoing(amplitudes, send_list[0])
-    received = lax.all_to_all(outgoing, "wide", split_axis=0, concat_axis=0, tiled=True)
+    head, tail = pick_outgoing(amplitudes, send_list[0], CUT)
+    head = lax.all_to_all(head, "wide", split_axis=0, concat_axis=0, tiled=True)
+    tail = lax.all_to_all(tail, "wide", split_axis=0, concat_axis=0, tiled=True)
     blocks = gather_integrals(integrals, n_nar)
     places = lax.all_gather(tile_positions, "narrow", axis=1, tiled=True)
-    return ladder(places, received, blocks)
+    return ladder(places, head, tail, blocks)
 
 
 def solution(mesh):

time: 168 us -> 157 us (0.935)
  the two profiles are of different devices: /device:TPU:76 before, /device:TPU:1 now
where the time goes in v6:
time: 157 us
  blocking collectives  73.8 us (47%)
  Pallas kernels  66.8 us (43%)
  starting transfers between devices  13.8 us (9%)
  local copies, waits for them, and re-layouts  2.07 us (1%)
    all_to_all x1, blocking collectives, on_device(): head = lax.all_to_all(head, 'wide', split_axis=0, concat_axis=0, tiled=True)  65.7 us
    pallas_call x1, Pallas kernels, gather_integrals(): pl.pallas_call(functools.partial(gather_kernel, n_nar), out_shape=jax.Sha...  52.7 us
    all_to_all x1, starting transfers between devices, on_device(): tail = lax.all_to_all(tail, 'wide', split_axis=0, concat_axis=0, tiled=True)  13.8 us
    pallas_call x1, Pallas kernels, ladder(): pl.pallas_call(functools.partial(ladder_kernel, n_x, n_k), out_shape=jax....  8.77 us
    all_gather x1, blocking collectives, on_device(): places = lax.all_gather(tile_positions, 'narrow', axis=1, tiled=True)  8.12 us
    pallas_call x1, Pallas kernels, pick_outgoing(): pl.pallas_call(functools.partial(pick_kernel, n_out, cut), out_shape=(jax...  5.32 us
  transfers between devices with their start and end apart: 1, of which 0 were waited for; matrix products, arithmetic and copies ran while one was open for 0% of the time, Pallas kernels for 34%

profile of v6, /device:TPU:1, one launch (start us, length us, event | category | flops | bytes accessed | tf_op | source)
XLA Modules:
  0.0 156.6 jit_solution(16563003672375955729)
XLA Ops:
  0.0 5.3 %shard_map.46 = (bf16[128,64,128]{2,1,0:T(8,128)(2,1)}, bf16[128,64,128]{2,1,0:T(8,128)(2,1)}) custom-call(s32[128]{0:T(128)} %bitcast.9, bf16[16,128,128]{2,1,0:T(8,128)(2,1)} %amp_ref.1), custom_call_target="tpu_custom_call" | custom-call | bytes 8388608 | tf_op jit(solution)/shard_map/pallas_call | solution.py:132
  5.3 65.7 %all_to_all.10.head_hbm = bf16[128,64,128]{2,1,0:T(8,128)(2,1)} all-to-all(bf16[128,64,128]{2,1,0:T(8,128)(2,1)} %get-tuple-element.7), channel_id=1, replica_groups=mesh['wide'=64,'narrow'=8] {'wide'}, dimensions={0} | all-to-all | bytes 4194304 | tf_op jit(solution)/shard_map/all_to_all | solution.py:147
  71.0 13.8 %all-to-all-start.1 = ((bf16[128,64,128]{2,1,0:T(8,128)(2,1)}), bf16[128,64,128]{2,1,0:T(8,128)(2,1)S(1)}, u32[]{:S(2)}, u32[]{:S(2)}) async-start(bf16[128,64,128]{2,1,0:T(8,128)(2,1)} %get-tuple-element.8), calls=%async_computation.1 | async-start | bytes 4194304 | tf_op jit(solution)/shard_map/all_to_all | solution.py:148
  84.8 0.0 copy-start.1
  84.9 52.7 %shard_map.47.blk_hbm = bf16[8,8,2,128,128]{4,3,2,1,0:T(8,128)(2,1)} custom-call(bf16[8,2,128,128]{3,2,1,0:T(8,128)(2,1)} %src_ref.1), custom_call_target="tpu_custom_call" | custom-call | bytes 8388608 | tf_op jit(solution)/shard_map/pallas_call | solution.py:47
  137.6 0.0 copy-done.1
  137.6 8.1 %all-gather = s32[8,2,8]{2,1,0:T(2,128)S(1)} all-gather(s32[1,2,8]{2,1,0:T(2,128)S(1)} %bitcast.8), channel_id=1, replica_groups=mesh['wide'=64,'narrow'=8] {'narrow'}, dimensions={0}, use_global_device_ids=true | all-gather | bytes 576 | tf_op jit(solution)/shard_map/all_gather | solution.py:150
  145.7 0.1 copy.6
  145.8 0.7 reshape.3.places_ref
  146.5 0.0 all-to-all-done.1.tail_hbm
  146.5 0.0 copy-start
  146.5 1.3 copy-done
  147.8 8.8 %shard_map.48 = bf16[8,128,128]{2,1,0:T(8,128)(2,1)} custom-call(s32[128]{0:T(128)} %reshape.3.places_ref, bf16[128,64,128]{2,1,0:T(8,128)(2,1)} %all_to_all.10.head_hbm, bf16[128,64,128]{2,1,0:T(8,128)(2,1)} %copy-done, bf16[8,8,2,128,128]{4,3,2,1,0:T(8,128)(2,1)} %shard_map.47.blk_hbm), custom_call_target="tpu_custom_call" | custom-call | flops 536870912 | bytes 8650752 | tf_op jit(solution)/shard_map/pallas_call | solution.py:95
Async XLA Ops:
  71.0 75.4 %all-to-all-start.1 = ((bf16[128,64,128]{2,1,0:T(8,128)(2,1)}), bf16[128,64,128]{2,1,0:T(8,128)(2,1)S(1)}, u32[]{:S(2)}, u32[]{:S(2)}) async-start(bf16[128,64,128]{2,1,0:T(8,128)(2,1)} %get-tuple-element.8), calls=%async_computation.1 | async-start | bytes 4194304 | tf_op jit(solution)/shard_map/all_to_all | solution.py:148
  84.8 52.7 %copy-start.1 = (s32[8,2]{0,1:T(2,128)S(1)}, s32[8,2]{0,1:T(2,128)}, u32[]{:S(2)}) copy-start(s32[8,2]{0,1:T(2,128)} %param.6) | copy-start | bytes 196
  146.5 1.3 copy-start

commit v7 on v6

--- a/solution.py
+++ b/solution.py
@@ -11,7 +11,7 @@
 CUT = 64
 
 
-def gather_kernel(n_nar, src_ref, dst_ref, send_sem, recv_sem, local_sem):
+def gather_kernel(n_nar, src_ref, pos_ref, dst_ref, pos_dst, send_sem, recv_sem, local_sem):
     me = lax.axis_index("narrow")
     w = lax.axis_index("wide")
 
@@ -21,52 +21,66 @@
         pl.semaphore_signal(barrier, 1, device_id=(w, peer), device_id_type=MESH)
     pl.semaphore_wait(barrier, n_nar - 1)
 
-    local = pltpu.make_async_copy(src_ref, dst_ref.at[me], local_sem)
-    local.start()
+    locals_ = [
+        pltpu.make_async_copy(src_ref, dst_ref.at[me], local_sem.at[0]),
+        pltpu.make_async_copy(pos_ref, pos_dst.at[me], local_sem.at[1]),
+    ]
+    for c in locals_:
+        c.start()
 
     def remote(peer, slot):
-        return pltpu.make_async_remote_copy(
-            src_ref=src_ref,
-            dst_ref=dst_ref.at[slot],
-            send_sem=send_sem.at[peer],
-            recv_sem=recv_sem.at[slot],
-            device_id=(w, peer),
-            device_id_type=MESH,
-        )
+        return [
+            pltpu.make_async_remote_copy(
+                src_ref=s,
+                dst_ref=d.at[slot],
+                send_sem=send_sem.at[part, peer],
+                recv_sem=recv_sem.at[part, slot],
+                device_id=(w, peer),
+                device_id_type=MESH,
+            )
+            for part, (s, d) in enumerate(((src_ref, dst_ref), (pos_ref, pos_dst)))
+        ]
 
     for i in range(1, n_nar):
-        remote(lax.rem(me + i, n_nar), me).start()
+        for c in remote(lax.rem(me + i, n_nar), me):
+            c.start()
     for i in range(1, n_nar):
-        remote(lax.rem(me + i, n_nar), me).wait_send()
+        for c in remote(lax.rem(me + i, n_nar), me):
+            c.wait_send()
         owner = lax.rem(me + n_nar - i, n_nar)
-        remote(owner, owner).wait_recv()
-    local.wait()
+        for c in remote(owner, owner):
+            c.wait_recv()
+    for c in locals_:
+        c.wait()
 
 
-def gather_integrals(integrals, n_nar):
+def gather_integrals(integrals, positions, n_nar):
     return pl.pallas_call(
         functools.partial(gather_kernel, n_nar),
-        out_shape=jax.ShapeDtypeStruct((n_nar,) + integrals.shape, integrals.dtype),
-        in_specs=[pl.BlockSpec(memory_space=pl.ANY)],
-        out_specs=pl.BlockSpec(memory_space=pl.ANY),
+        out_shape=(
+            jax.ShapeDtypeStruct((n_nar,) + integrals.shape, integrals.dtype),
+            jax.ShapeDtypeStruct((n_nar,) + positions.shape, positions.dtype),
+        ),
+        in_specs=[pl.BlockSpec(memory_space=pl.ANY), pl.BlockSpec(memory_space=pl.ANY)],
+        out_specs=(pl.BlockSpec(memory_space=pl.ANY), pl.BlockSpec(memory_space=pl.ANY)),
         scratch_shapes=[
-            pltpu.SemaphoreType.DMA((n_nar,)),
-            pltpu.SemaphoreType.DMA((n_nar,)),
-            pltpu.SemaphoreType.DMA,
+            pltpu.SemaphoreType.DMA((2, n_nar)),
+            pltpu.SemaphoreType.DMA((2, n_nar)),
+            pltpu.SemaphoreType.DMA((2,)),
         ],
         compiler_params=pltpu.CompilerParams(collective_id=0, has_side_effects=True),
         cost_estimate=pl.CostEstimate(
             flops=0, transcendentals=0, bytes_accessed=2 * n_nar * integrals.size * 2
         ),
-    )(integrals)
+    )(integrals, positions)
 
 
-def ladder_kernel(n_x, n_k, places_ref, head_hbm, tail_hbm, blk_hbm, out_ref, tiles, blks, sems):
+def ladder_kernel(n_x, n_k, per, places_ref, head_hbm, tail_hbm, blk_hbm, out_ref, tiles, blks, sems):
     def copies(x, slot):
         cut = head_hbm.shape[1]
         picked = []
         for k in range(n_k):
-            p = places_ref[x * n_k + k]
+            p = places_ref[k // per, x, k % per]
             dst = tiles.at[slot, k]
             picked.append(pltpu.make_async_copy(head_hbm.at[p], dst.at[pl.ds(0, cut)], sems.at[slot, 0, k]))
             picked.append(
@@ -93,7 +107,7 @@
     n_k = n_nar * per
     rows = head.shape[1] + tail.shape[1]
     return pl.pallas_call(
-        functools.partial(ladder_kernel, n_x, n_k),
+        functools.partial(ladder_kernel, n_x, n_k, per),
         out_shape=jax.ShapeDtypeStruct((n_x, rows, s), jnp.bfloat16),
         in_specs=[
             pl.BlockSpec(memory_space=pltpu.SMEM),
@@ -112,7 +126,7 @@
             transcendentals=0,
             bytes_accessed=2 * (2 * blocks.size + n_x * rows * s),
         ),
-    )(places.reshape(-1), head, tail, blocks)
+    )(places, head, tail, blocks)
 
 
 def pick_kernel(n_out, cut, sel_ref, amp_ref, head_hbm, tail_hbm, sems):
@@ -146,8 +160,9 @@
     head, tail = pick_outgoing(amplitudes, send_list[0], CUT)
     head = lax.all_to_all(head, "wide", split_axis=0, concat_axis=0, tiled=True)
     tail = lax.all_to_all(tail, "wide", split_axis=0, concat_axis=0, tiled=True)
-    blocks = gather_integrals(integrals, n_nar)
-    places = lax.all_gather(tile_positions, "narrow", axis=1, tiled=True)
+    lanes = jnp.zeros((tile_positions.shape[0], 128), tile_positions.dtype)
+    lanes = lax.dynamic_update_slice(lanes, tile_positions, (0, 0))
+    blocks, places = gather_integrals(integrals, lanes, n_nar)
     return ladder(places, head, tail, blocks)
 
 

time: 157 us -> 150 us (0.955)
  the two profiles are of different devices: /device:TPU:1 before, /device:TPU:30 now
where the time goes in v7:
time: 150 us
  blocking collectives  70.6 us (47%)
  Pallas kernels  63.3 us (42%)
  starting transfers between devices  9.2 us (6%)
  waiting for transfers between devices  4.59 us (3%)
  local copies, waits for them, and re-layouts  2.04 us (1%)
    all_to_all x1, blocking collectives, on_device(): head = lax.all_to_all(head, 'wide', split_axis=0, concat_axis=0, tiled=True)  70.6 us
    pallas_call x1, Pallas kernels, gather_integrals(): pl.pallas_call(functools.partial(gather_kernel, n_nar), out_shape=(jax.Sh...  48.7 us
    pallas_call x1, Pallas kernels, ladder(): pl.pallas_call(functools.partial(ladder_kernel, n_x, n_k, per), out_shape...  9.3 us
    all_to_all x1, starting transfers between devices, on_device(): tail = lax.all_to_all(tail, 'wide', split_axis=0, concat_axis=0, tiled=True)  9.2 us
    pallas_call x1, Pallas kernels, pick_outgoing(): pl.pallas_call(functools.partial(pick_kernel, n_out, cut), out_shape=(jax...  5.32 us
    all_to_all x1, waiting for transfers between devices, on_device(): tail = lax.all_to_all(tail, 'wide', split_axis=0, concat_axis=0, tiled=True)  4.59 us
  transfers between devices with their start and end apart: 1, of which 1 were waited for; matrix products, arithmetic and copies ran while one was open for 0% of the time, Pallas kernels for 32%

profile of v7, /device:TPU:30, one launch (start us, length us, event | category | flops | bytes accessed | tf_op | source)
XLA Modules:
  0.0 149.8 jit_solution(7099133745816477821)
XLA Ops:
  0.0 5.3 %shard_map.47 = (bf16[128,64,128]{2,1,0:T(8,128)(2,1)}, bf16[128,64,128]{2,1,0:T(8,128)(2,1)}) custom-call(s32[128]{0:T(128)} %bitcast.1, bf16[16,128,128]{2,1,0:T(8,128)(2,1)} %amp_ref.1), custom_call_target="tpu_custom_call" | custom-call | bytes 8388608 | tf_op jit(solution)/shard_map/pallas_call | solution.py:146
  5.3 70.6 %all_to_all.10.head_hbm = bf16[128,64,128]{2,1,0:T(8,128)(2,1)} all-to-all(bf16[128,64,128]{2,1,0:T(8,128)(2,1)} %get-tuple-element.10), channel_id=1, replica_groups=mesh['wide'=64,'narrow'=8] {'wide'}, dimensions={0} | all-to-all | bytes 4194304 | tf_op jit(solution)/shard_map/all_to_all | solution.py:161
  76.0 0.0 copy-start.1
  76.0 9.2 %all-to-all-start.1 = ((bf16[128,64,128]{2,1,0:T(8,128)(2,1)}), bf16[128,64,128]{2,1,0:T(8,128)(2,1)S(1)}, u32[]{:S(2)}, u32[]{:S(2)}) async-start(bf16[128,64,128]{2,1,0:T(8,128)(2,1)} %get-tuple-element.11), calls=%async_computation.1 | async-start | bytes 4194304 | tf_op jit(solution)/shard_map/all_to_all | solution.py:162
  85.2 0.0 copy-done.1
  85.2 0.1 copy.5
  85.3 0.6 dynamic_update_slice.3.pos_ref
  85.9 48.7 %shard_map.46 = (bf16[8,8,2,128,128]{4,3,2,1,0:T(8,128)(2,1)}, s32[8,8,128]{2,1,0:T(8,128)}) custom-call(bf16[8,2,128,128]{3,2,1,0:T(8,128)(2,1)} %src_ref.1, s32[8,128]{1,0:T(8,128)} %dynamic_update_slice.3.pos_ref), custom_call_target="tpu_custom_call" | custom-call | bytes 8388608 | tf_op jit(solution)/shard_map/pallas_call | solution.py:58
  134.5 4.6 %all-to-all-done.1.tail_hbm = bf16[128,64,128]{2,1,0:T(8,128)(2,1)S(1)} async-done(((bf16[128,64,128]{2,1,0:T(8,128)(2,1)}), bf16[128,64,128]{2,1,0:T(8,128)(2,1)S(1)}, u32[]{:S(2)}, u32[]{:S(2)}) %all-to-all-start.1) | async-done | bytes 2097184 | tf_op jit(solution)/shard_map/all_to_all | solution.py:162
  139.1 0.0 copy-start
  139.1 1.3 copy-done
  140.5 9.3 %shard_map.48 = bf16[8,128,128]{2,1,0:T(8,128)(2,1)} custom-call(s32[8,8,128]{2,1,0:T(8,128)} %get-tuple-element.9.places_ref, bf16[128,64,128]{2,1,0:T(8,128)(2,1)} %all_to_all.10.head_hbm, bf16[128,64,128]{2,1,0:T(8,128)(2,1)} %copy-done, bf16[8,8,2,128,128]{4,3,2,1,0:T(8,128)(2,1)} %get-tuple-element.12.blk_hbm), custom_call_target="tpu_custom_call" | custom-call | flops 536870912 | bytes 8650752 | tf_op jit(solution)/shard_map/pallas_call | solution.py:109
Async XLA Ops:
  76.0 9.2 %copy-start.1 = (s32[8,2]{0,1:T(2,128)S(1)}, s32[8,2]{0,1:T(2,128)}, u32[]{:S(2)}) copy-start(s32[8,2]{0,1:T(2,128)} %param.6) | copy-start | bytes 196
  76.0 63.2 %all-to-all-start.1 = ((bf16[128,64,128]{2,1,0:T(8,128)(2,1)}), bf16[128,64,128]{2,1,0:T(8,128)(2,1)S(1)}, u32[]{:S(2)}, u32[]{:S(2)}) async-start(bf16[128,64,128]{2,1,0:T(8,128)(2,1)} %get-tuple-element.11), calls=%async_computation.1 | async-start | bytes 4194304 | tf_op jit(solution)/shard_map/all_to_all | solution.py:162
  139.1 1.4 copy-start

commit v8 on v7

--- a/solution.py
+++ b/solution.py
@@ -8,7 +8,7 @@
 from jax.sharding import PartitionSpec as P
 
 MESH = pl.DeviceIdType.MESH
-CUT = 64
+CUT = 48
 
 
 def gather_kernel(n_nar, src_ref, pos_ref, dst_ref, pos_dst, send_sem, recv_sem, local_sem):

time: 150 us -> 150 us (level)
  the two profiles are of different devices: /device:TPU:30 before, /device:TPU:158 now
where the time goes in v8:
time: 150 us
  Pallas kernels  63.3 us (42%)
  blocking collectives  55.1 us (37%)
  waiting for transfers between devices  20 us (13%)
  starting transfers between devices  8.98 us (6%)
  local copies, waits for them, and re-layouts  2.22 us (1%)
    all_to_all x1, blocking collectives, on_device(): head = lax.all_to_all(head, 'wide', split_axis=0, concat_axis=0, tiled=True)  55.1 us
    pallas_call x1, Pallas kernels, gather_integrals(): pl.pallas_call(functools.partial(gather_kernel, n_nar), out_shape=(jax.Sh...  48.7 us
    all_to_all x1, waiting for transfers between devices, on_device(): tail = lax.all_to_all(tail, 'wide', split_axis=0, concat_axis=0, tiled=True)  20 us
    pallas_call x1, Pallas kernels, ladder(): pl.pallas_call(functools.partial(ladder_kernel, n_x, n_k, per), out_shape...  9.31 us
    all_to_all x1, starting transfers between devices, on_device(): tail = lax.all_to_all(tail, 'wide', split_axis=0, concat_axis=0, tiled=True)  8.98 us
    pallas_call x1, Pallas kernels, pick_outgoing(): pl.pallas_call(functools.partial(pick_kernel, n_out, cut), out_shape=(jax...  5.28 us
  transfers between devices with their start and end apart: 1, of which 1 were waited for; matrix products, arithmetic and copies ran while one was open for 0% of the time, Pallas kernels for 33%

profile of v8, /device:TPU:158, one launch (start us, length us, event | category | flops | bytes accessed | tf_op | source)
XLA Modules:
  0.0 149.5 jit_solution(6740197943073172761)
XLA Ops:
  0.0 5.3 %shard_map.47 = (bf16[128,48,128]{2,1,0:T(8,128)(2,1)}, bf16[128,80,128]{2,1,0:T(8,128)(2,1)}) custom-call(s32[128]{0:T(128)} %bitcast.1, bf16[16,128,128]{2,1,0:T(8,128)(2,1)} %amp_ref.1), custom_call_target="tpu_custom_call" | custom-call | bytes 8388608 | tf_op jit(solution)/shard_map/pallas_call | solution.py:146
  5.3 55.1 %all_to_all.10.head_hbm = bf16[128,48,128]{2,1,0:T(8,128)(2,1)} all-to-all(bf16[128,48,128]{2,1,0:T(8,128)(2,1)} %get-tuple-element.10), channel_id=1, replica_groups=mesh['wide'=64,'narrow'=8] {'wide'}, dimensions={0} | all-to-all | bytes 3145728 | tf_op jit(solution)/shard_map/all_to_all | solution.py:161
  60.3 0.0 copy-start.1
  60.3 9.0 %all-to-all-start.1 = ((bf16[128,80,128]{2,1,0:T(8,128)(2,1)}), bf16[128,80,128]{2,1,0:T(8,128)(2,1)S(1)}, u32[]{:S(2)}, u32[]{:S(2)}) async-start(bf16[128,80,128]{2,1,0:T(8,128)(2,1)} %get-tuple-element.11), calls=%async_computation.1 | async-start | bytes 5242880 | tf_op jit(solution)/shard_map/all_to_all | solution.py:162
  69.3 0.0 copy-done.1
  69.3 0.1 copy.5
  69.4 0.6 dynamic_update_slice.3.pos_ref
  70.0 48.7 %shard_map.46 = (bf16[8,8,2,128,128]{4,3,2,1,0:T(8,128)(2,1)}, s32[8,8,128]{2,1,0:T(8,128)}) custom-call(bf16[8,2,128,128]{3,2,1,0:T(8,128)(2,1)} %src_ref.1, s32[8,128]{1,0:T(8,128)} %dynamic_update_slice.3.pos_ref), custom_call_target="tpu_custom_call" | custom-call | bytes 8388608 | tf_op jit(solution)/shard_map/pallas_call | solution.py:58
  118.7 20.0 %all-to-all-done.1.tail_hbm = bf16[128,80,128]{2,1,0:T(8,128)(2,1)S(1)} async-done(((bf16[128,80,128]{2,1,0:T(8,128)(2,1)}), bf16[128,80,128]{2,1,0:T(8,128)(2,1)S(1)}, u32[]{:S(2)}, u32[]{:S(2)}) %all-to-all-start.1) | async-done | bytes 2621472 | tf_op jit(solution)/shard_map/all_to_all | solution.py:162
  138.7 0.0 copy-start
  138.7 1.5 %copy-done = bf16[128,80,128]{2,1,0:T(8,128)(2,1)} copy-done((bf16[128,80,128]{2,1,0:T(8,128)(2,1)}, bf16[128,80,128]{2,1,0:T(8,128)(2,1)S(1)}, u32[]{:S(2)}) %copy-start) | copy-done | bytes 2621464
  140.2 9.3 %shard_map.48 = bf16[8,128,128]{2,1,0:T(8,128)(2,1)} custom-call(s32[8,8,128]{2,1,0:T(8,128)} %get-tuple-element.9.places_ref, bf16[128,48,128]{2,1,0:T(8,128)(2,1)} %all_to_all.10.head_hbm, bf16[128,80,128]{2,1,0:T(8,128)(2,1)} %copy-done, bf16[8,8,2,128,128]{4,3,2,1,0:T(8,128)(2,1)} %get-tuple-element.12.blk_hbm), custom_call_target="tpu_custom_call" | custom-call | flops 536870912 | bytes 8650752 | tf_op jit(solution)/shard_map/pallas_call | solution.py:109
Async XLA Ops:
  60.3 9.0 %copy-start.1 = (s32[8,2]{0,1:T(2,128)S(1)}, s32[8,2]{0,1:T(2,128)}, u32[]{:S(2)}) copy-start(s32[8,2]{0,1:T(2,128)} %param.6) | copy-start | bytes 196
  60.3 78.3 %all-to-all-start.1 = ((bf16[128,80,128]{2,1,0:T(8,128)(2,1)}), bf16[128,80,128]{2,1,0:T(8,128)(2,1)S(1)}, u32[]{:S(2)}, u32[]{:S(2)}) async-start(bf16[128,80,128]{2,1,0:T(8,128)(2,1)} %get-tuple-element.11), calls=%async_computation.1 | async-start | bytes 5242880 | tf_op jit(solution)/shard_map/all_to_all | solution.py:162
  138.7 1.5 %copy-start = (bf16[128,80,128]{2,1,0:T(8,128)(2,1)}, bf16[128,80,128]{2,1,0:T(8,128)(2,1)S(1)}, u32[]{:S(2)}) copy-start(bf16[128,80,128]{2,1,0:T(8,128)(2,1)S(1)} %all-to-all-done.1.tail_hbm) | copy-start | bytes 7864324

commit v9 on v8

--- a/solution.py
+++ b/solution.py
@@ -73,6 +73,84 @@
             flops=0, transcendentals=0, bytes_accessed=2 * n_nar * integrals.size * 2
         ),
     )(integrals, positions)
+
+
+def ladder_kernel(n_x, n_k, per, places_ref, head_hbm, tail_hbm, blk_hbm, out_ref, tiles, blks, sems):
+    def copies(x, slot):
+        cut = head_hbm.shape[1]
+        picked = []
+        for k in range(n_k):
+            p = places_ref[k // per, x, k % per]
+            dst = tiles.at[slot, k]
+            picked.append(pltpu.make_async_copy(head_hbm.at[p], dst.at[pl.ds(0, cut)], sems.at[slot, 0, k]))
+            picked.append(
+                pltpu.make_async_copy(tail_hbm.at[p], dst.at[pl.ds(cut, dst.shape[0] - cut)], sems.at[slot, 1, k])
+            )
+        return picked + [pltpu.make_async_copy(blk_hbm.at[:, x], blks.at[slot], sems.at[slot, 2, 0])]
+
+    for c in copies(0, 0):
+        c.start()
+    for x in range(n_x):
+        slot = x % 2
+        if x + 1 < n_x:
+            for c in copies(x + 1, 1 - slot):
+                c.start()
+        for c in copies(x, slot):
+            c.wait()
+        lhs = jnp.concatenate([tiles[slot, k] for k in range(n_k)], axis=1)
+        rhs = blks[slot].reshape(n_k * blks.shape[-2], blks.shape[-1])
+        out_ref[x] = jnp.dot(lhs, rhs, preferred_element_type=jnp.float32).astype(out_ref.dtype)
+
+
+def ladder(places, head, tail, blocks):
+    n_nar, n_x, per, t, s = blocks.shape
+    n_k = n_nar * per
+    rows = head.shape[1] + tail.shape[1]
+    return pl.pallas_call(
+        functools.partial(ladder_kernel, n_x, n_k, per),
+        out_shape=jax.ShapeDtypeStruct((n_x, rows, s), jnp.bfloat16),
+        in_specs=[
+            pl.BlockSpec(memory_space=pltpu.SMEM),
+            pl.BlockSpec(memory_space=pl.ANY),
+            pl.BlockSpec(memory_space=pl.ANY),
+            pl.BlockSpec(memory_space=pl.ANY),
+        ],
+        out_specs=pl.BlockSpec(memory_space=pltpu.VMEM),
+        scratch_shapes=[
+            pltpu.VMEM((2, n_k, rows, t), head.dtype),
+            pltpu.VMEM((2, n_nar, per, t, s), blocks.dtype),
+            pltpu.SemaphoreType.DMA((2, 3, n_k)),
+        ],
+        cost_estimate=pl.CostEstimate(
+            flops=2 * n_x * n_k * rows * t * s,
+            transcendentals=0,
+            bytes_accessed=2 * (2 * blocks.size + n_x * rows * s),
+        ),
+    )(places, head, tail, blocks)
+
+
+def pick_kernel(n_out, cut, sel_ref, amp_ref, head_ref, tail_ref):
+    def body(j, carry):
+        tile = amp_ref[sel_ref[j]]
+        head_ref[j] = tile[:cut]
+        tail_ref[j] = tile[cut:]
+        return carry
+
+    lax.fori_loop(0, n_out, body, 0)
+
+
+def pick_outgoing(amplitudes, selection, cut):
+    n_out, (rows, t) = selection.shape[0], amplitudes.shape[1:]
+    return pl.pallas_call(
+        functools.partial(pick_kernel, n_out, cut),
+        out_shape=(
+            jax.ShapeDtypeStruct((n_out, cut, t), amplitudes.dtype),
+            jax.ShapeDtypeStruct((n_out, rows - cut, t), amplitudes.dtype),
+        ),
+        in_specs=[pl.BlockSpec(memory_space=pltpu.SMEM), pl.BlockSpec(memory_space=pltpu.VMEM)],
+        out_specs=(pl.BlockSpec(memory_space=pltpu.VMEM), pl.BlockSpec(memory_space=pltpu.VMEM)),
+        cost_estimate=pl.CostEstimate(flops=0, transcendentals=0, bytes_accessed=4 * n_out * amplitudes[0].size),
+    )(selection, amplitudes)
 
 
 def ladder_kernel(n_x, n_k, per, places_ref, head_hbm, tail_hbm, blk_hbm, out_ref, tiles, blks, sems):

time: 150 us -> 150 us (level)
  no operation moved by 1% of the time
where the time goes in v9:
time: 150 us
  Pallas kernels  63.3 us (42%)
  blocking collectives  55.1 us (37%)
  waiting for transfers between devices  20 us (13%)
  starting transfers between devices  8.98 us (6%)
  local copies, waits for them, and re-layouts  2.22 us (1%)
    all_to_all x1, blocking collectives, on_device(): head = lax.all_to_all(head, 'wide', split_axis=0, concat_axis=0, tiled=True)  55.1 us
    pallas_call x1, Pallas kernels, gather_integrals(): pl.pallas_call(functools.partial(gather_kernel, n_nar), out_shape=(jax.Sh...  48.7 us
    all_to_all x1, waiting for transfers between devices, on_device(): tail = lax.all_to_all(tail, 'wide', split_axis=0, concat_axis=0, tiled=True)  20 us
    pallas_call x1, Pallas kernels, ladder(): pl.pallas_call(functools.partial(ladder_kernel, n_x, n_k, per), out_shape...  9.31 us
    all_to_all x1, starting transfers between devices, on_device(): tail = lax.all_to_all(tail, 'wide', split_axis=0, concat_axis=0, tiled=True)  8.98 us
    pallas_call x1, Pallas kernels, pick_outgoing(): pl.pallas_call(functools.partial(pick_kernel, n_out, cut), out_shape=(jax...  5.28 us
  transfers between devices with their start and end apart: 1, of which 1 were waited for; matrix products, arithmetic and copies ran while one was open for 0% of the time, Pallas kernels for 33%

profile of v9, /device:TPU:158, one launch (start us, length us, event | category | flops | bytes accessed | tf_op | source)
XLA Modules:
  0.0 149.5 jit_solution(6740197943073172761)
XLA Ops:
  0.0 5.3 %shard_map.47 = (bf16[128,48,128]{2,1,0:T(8,128)(2,1)}, bf16[128,80,128]{2,1,0:T(8,128)(2,1)}) custom-call(s32[128]{0:T(128)} %bitcast.1, bf16[16,128,128]{2,1,0:T(8,128)(2,1)} %amp_ref.1), custom_call_target="tpu_custom_call" | custom-call | bytes 8388608 | tf_op jit(solution)/shard_map/pallas_call | solution.py:224
  5.3 55.1 %all_to_all.10.head_hbm = bf16[128,48,128]{2,1,0:T(8,128)(2,1)} all-to-all(bf16[128,48,128]{2,1,0:T(8,128)(2,1)} %get-tuple-element.10), channel_id=1, replica_groups=mesh['wide'=64,'narrow'=8] {'wide'}, dimensions={0} | all-to-all | bytes 3145728 | tf_op jit(solution)/shard_map/all_to_all | solution.py:239
  60.3 0.0 copy-start.1
  60.3 9.0 %all-to-all-start.1 = ((bf16[128,80,128]{2,1,0:T(8,128)(2,1)}), bf16[128,80,128]{2,1,0:T(8,128)(2,1)S(1)}, u32[]{:S(2)}, u32[]{:S(2)}) async-start(bf16[128,80,128]{2,1,0:T(8,128)(2,1)} %get-tuple-element.11), calls=%async_computation.1 | async-start | bytes 5242880 | tf_op jit(solution)/shard_map/all_to_all | solution.py:240
  69.3 0.0 copy-done.1
  69.3 0.1 copy.5
  69.4 0.6 dynamic_update_slice.3.pos_ref
  70.0 48.7 %shard_map.46 = (bf16[8,8,2,128,128]{4,3,2,1,0:T(8,128)(2,1)}, s32[8,8,128]{2,1,0:T(8,128)}) custom-call(bf16[8,2,128,128]{3,2,1,0:T(8,128)(2,1)} %src_ref.1, s32[8,128]{1,0:T(8,128)} %dynamic_update_slice.3.pos_ref), custom_call_target="tpu_custom_call" | custom-call | bytes 8388608 | tf_op jit(solution)/shard_map/pallas_call | solution.py:58
  118.7 20.0 %all-to-all-done.1.tail_hbm = bf16[128,80,128]{2,1,0:T(8,128)(2,1)S(1)} async-done(((bf16[128,80,128]{2,1,0:T(8,128)(2,1)}), bf16[128,80,128]{2,1,0:T(8,128)(2,1)S(1)}, u32[]{:S(2)}, u32[]{:S(2)}) %all-to-all-start.1) | async-done | bytes 2621472 | tf_op jit(solution)/shard_map/all_to_all | solution.py:240
  138.7 0.0 copy-start
  138.7 1.5 %copy-done = bf16[128,80,128]{2,1,0:T(8,128)(2,1)} copy-done((bf16[128,80,128]{2,1,0:T(8,128)(2,1)}, bf16[128,80,128]{2,1,0:T(8,128)(2,1)S(1)}, u32[]{:S(2)}) %copy-start) | copy-done | bytes 2621464
  140.2 9.3 %shard_map.48 = bf16[8,128,128]{2,1,0:T(8,128)(2,1)} custom-call(s32[8,8,128]{2,1,0:T(8,128)} %get-tuple-element.9.places_ref, bf16[128,48,128]{2,1,0:T(8,128)(2,1)} %all_to_all.10.head_hbm, bf16[128,80,128]{2,1,0:T(8,128)(2,1)} %copy-done, bf16[8,8,2,128,128]{4,3,2,1,0:T(8,128)(2,1)} %get-tuple-element.12.blk_hbm), custom_call_target="tpu_custom_call" | custom-call | flops 536870912 | bytes 8650752 | tf_op jit(solution)/shard_map/pallas_call | solution.py:187
Async XLA Ops:
  60.3 9.0 %copy-start.1 = (s32[8,2]{0,1:T(2,128)S(1)}, s32[8,2]{0,1:T(2,128)}, u32[]{:S(2)}) copy-start(s32[8,2]{0,1:T(2,128)} %param.6) | copy-start | bytes 196
  60.3 78.3 %all-to-all-start.1 = ((bf16[128,80,128]{2,1,0:T(8,128)(2,1)}), bf16[128,80,128]{2,1,0:T(8,128)(2,1)S(1)}, u32[]{:S(2)}, u32[]{:S(2)}) async-start(bf16[128,80,128]{2,1,0:T(8,128)(2,1)} %get-tuple-element.11), calls=%async_computation.1 | async-start | bytes 5242880 | tf_op jit(solution)/shard_map/all_to_all | solution.py:240
  138.7 1.5 %copy-start = (bf16[128,80,128]{2,1,0:T(8,128)(2,1)}, bf16[128,80,128]{2,1,0:T(8,128)(2,1)S(1)}, u32[]{:S(2)}) copy-start(bf16[128,80,128]{2,1,0:T(8,128)(2,1)S(1)} %all-to-all-done.1.tail_hbm) | copy-start | bytes 7864324

commit v10 on v8

--- a/solution.py
+++ b/solution.py
@@ -75,18 +75,15 @@
     )(integrals, positions)
 
 
-def ladder_kernel(n_x, n_k, per, places_ref, head_hbm, tail_hbm, blk_hbm, out_ref, tiles, blks, sems):
+def ladder_kernel(n_x, n_k, per, places_ref, recv_hbm, blk_hbm, out_ref, tiles, blks, sems):
     def copies(x, slot):
-        cut = head_hbm.shape[1]
-        picked = []
-        for k in range(n_k):
-            p = places_ref[k // per, x, k % per]
-            dst = tiles.at[slot, k]
-            picked.append(pltpu.make_async_copy(head_hbm.at[p], dst.at[pl.ds(0, cut)], sems.at[slot, 0, k]))
-            picked.append(
-                pltpu.make_async_copy(tail_hbm.at[p], dst.at[pl.ds(cut, dst.shape[0] - cut)], sems.at[slot, 1, k])
+        picked = [
+            pltpu.make_async_copy(
+                recv_hbm.at[places_ref[k // per, x, k % per]], tiles.at[slot, k], sems.at[slot, k]
             )
-        return picked + [pltpu.make_async_copy(blk_hbm.at[:, x], blks.at[slot], sems.at[slot, 2, 0])]
+            for k in range(n_k)
+        ]
+        return picked + [pltpu.make_async_copy(blk_hbm.at[:, x], blks.at[slot], sems.at[slot, n_k])]
 
     for c in copies(0, 0):
         c.start()
@@ -102,10 +99,10 @@
         out_ref[x] = jnp.dot(lhs, rhs, preferred_element_type=jnp.float32).astype(out_ref.dtype)
 
 
-def ladder(places, head, tail, blocks):
+def ladder(places, received, blocks):
     n_nar, n_x, per, t, s = blocks.shape
     n_k = n_nar * per
-    rows = head.shape[1] + tail.shape[1]
+    rows = received.shape[1]
     return pl.pallas_call(
         functools.partial(ladder_kernel, n_x, n_k, per),
         out_shape=jax.ShapeDtypeStruct((n_x, rows, s), jnp.bfloat16),
@@ -113,20 +110,19 @@
             pl.BlockSpec(memory_space=pltpu.SMEM),
             pl.BlockSpec(memory_space=pl.ANY),
             pl.BlockSpec(memory_space=pl.ANY),
-            pl.BlockSpec(memory_space=pl.ANY),
         ],
         out_specs=pl.BlockSpec(memory_space=pltpu.VMEM),
         scratch_shapes=[
-            pltpu.VMEM((2, n_k, rows, t), head.dtype),
+            pltpu.VMEM((2, n_k, rows, t), received.dtype),
             pltpu.VMEM((2, n_nar, per, t, s), blocks.dtype),
-            pltpu.SemaphoreType.DMA((2, 3, n_k)),
+            pltpu.SemaphoreType.DMA((2, n_k + 1)),
         ],
         cost_estimate=pl.CostEstimate(
             flops=2 * n_x * n_k * rows * t * s,
             transcendentals=0,
             bytes_accessed=2 * (2 * blocks.size + n_x * rows * s),
         ),
-    )(places, head, tail, blocks)
+    )(places, received, blocks)
 
 
 def pick_kernel(n_out, cut, sel_ref, amp_ref, head_hbm, tail_hbm, sems):
@@ -163,7 +159,8 @@
     lanes = jnp.zeros((tile_positions.shape[0], 128), tile_positions.dtype)
     lanes = lax.dynamic_update_slice(lanes, tile_positions, (0, 0))
     blocks, places = gather_integrals(integrals, lanes, n_nar)
-    return ladder(places, head, tail, blocks)
+    rows = [ladder(places, part, blocks) for part in (head, tail)]
+    return jnp.concatenate(rows, axis=1)
 
 
 def solution(mesh):

time: 150 us -> 151 us (level)
  the two profiles are of different devices: /device:TPU:158 before, /device:TPU:152 now
where the time goes in v10:
time: 151 us; the launch traced here: 150 us
  Pallas kernels  71.4 us (47%)
  blocking collectives  55.1 us (36%)
  waiting for transfers between devices  10.5 us (7%)
  starting transfers between devices  8.98 us (6%)
  local copies, waits for them, and re-layouts  2.22 us (1%)
  other arithmetic  1.64 us (1%)
    all_to_all x1, blocking collectives, on_device(): head = lax.all_to_all(head, 'wide', split_axis=0, concat_axis=0, tiled=True)  55.1 us
    pallas_call x1, Pallas kernels, gather_integrals(): pl.pallas_call(functools.partial(gather_kernel, n_nar), out_shape=(jax.Sh...  50.3 us
    pallas_call x2, Pallas kernels, ladder(): pl.pallas_call(functools.partial(ladder_kernel, n_x, n_k, per), out_shape...  15.9 us
    all_to_all x1, waiting for transfers between devices, on_device(): tail = lax.all_to_all(tail, 'wide', split_axis=0, concat_axis=0, tiled=True)  10.5 us
    all_to_all x1, starting transfers between devices, on_device(): tail = lax.all_to_all(tail, 'wide', split_axis=0, concat_axis=0, tiled=True)  8.98 us
    pallas_call x1, Pallas kernels, pick_outgoing(): pl.pallas_call(functools.partial(pick_kernel, n_out, cut), out_shape=(jax...  5.27 us
  transfers between devices with their start and end apart: 1, of which 1 were waited for; matrix products, arithmetic and copies ran while one was open for 0% of the time, Pallas kernels for 39%

profile of v10, /device:TPU:152, one launch (start us, length us, event | category | flops | bytes accessed | tf_op | source)
XLA Modules:
  0.0 149.9 jit_solution(1566936846071552763)
XLA Ops:
  0.0 5.3 %shard_map.47 = (bf16[128,48,128]{2,1,0:T(8,128)(2,1)}, bf16[128,80,128]{2,1,0:T(8,128)(2,1)}) custom-call(s32[128]{0:T(128)} %bitcast.1, bf16[16,128,128]{2,1,0:T(8,128)(2,1)} %amp_ref.1), custom_call_target="tpu_custom_call" | custom-call | bytes 8388608 | tf_op jit(solution)/shard_map/pallas_call | solution.py:142
  5.3 55.1 %all_to_all.10.recv_hbm = bf16[128,48,128]{2,1,0:T(8,128)(2,1)} all-to-all(bf16[128,48,128]{2,1,0:T(8,128)(2,1)} %get-tuple-element.10), channel_id=1, replica_groups=mesh['wide'=64,'narrow'=8] {'wide'}, dimensions={0} | all-to-all | bytes 3145728 | tf_op jit(solution)/shard_map/all_to_all | solution.py:157
  60.3 0.0 copy-start.2
  60.3 9.0 %all-to-all-start.1 = ((bf16[128,80,128]{2,1,0:T(8,128)(2,1)}), bf16[128,80,128]{2,1,0:T(8,128)(2,1)S(1)}, u32[]{:S(2)}, u32[]{:S(2)}) async-start(bf16[128,80,128]{2,1,0:T(8,128)(2,1)} %get-tuple-element.12), calls=%async_computation.1 | async-start | bytes 5242880 | tf_op jit(solution)/shard_map/all_to_all | solution.py:158
  69.3 0.0 copy-done.2
  69.3 0.1 copy.5
  69.4 0.6 dynamic_update_slice.3.pos_ref
  70.0 50.3 %shard_map.46 = (bf16[8,8,2,128,128]{4,3,2,1,0:T(8,128)(2,1)}, s32[8,8,128]{2,1,0:T(8,128)}) custom-call(bf16[8,2,128,128]{3,2,1,0:T(8,128)(2,1)} %src_ref.1, s32[8,128]{1,0:T(8,128)} %dynamic_update_slice.3.pos_ref), custom_call_target="tpu_custom_call" | custom-call | bytes 8388608 | tf_op jit(solution)/shard_map/pallas_call | solution.py:58
  120.3 7.8 %shard_map.48 = bf16[8,48,128]{2,1,0:T(8,128)(2,1)} custom-call(s32[8,8,128]{2,1,0:T(8,128)} %get-tuple-element.9.places_ref, bf16[128,48,128]{2,1,0:T(8,128)(2,1)} %all_to_all.10.recv_hbm, bf16[8,8,2,128,128]{4,3,2,1,0:T(8,128)(2,1)} %get-tuple-element.11.blk_hbm), custom_call_target="tpu_custom_call" | custom-call | flops 201326592 | bytes 8486912 | tf_op jit(solution)/shard_map/pallas_call | solution.py:106
  128.1 0.0 copy-start.1
  128.1 10.5 %all-to-all-done.1.recv_hbm = bf16[128,80,128]{2,1,0:T(8,128)(2,1)S(1)} async-done(((bf16[128,80,128]{2,1,0:T(8,128)(2,1)}), bf16[128,80,128]{2,1,0:T(8,128)(2,1)S(1)}, u32[]{:S(2)}, u32[]{:S(2)}) %all-to-all-start.1) | async-done | bytes 2621472 | tf_op jit(solution)/shard_map/all_to_all | solution.py:158
  138.7 0.0 copy-start
  138.7 1.5 %copy-done = bf16[128,80,128]{2,1,0:T(8,128)(2,1)} copy-done((bf16[128,80,128]{2,1,0:T(8,128)(2,1)}, bf16[128,80,128]{2,1,0:T(8,128)(2,1)S(1)}, u32[]{:S(2)}) %copy-start) | copy-done | bytes 2621464
  140.2 8.1 %shard_map.49 = bf16[8,80,128]{2,1,0:T(8,128)(2,1)} custom-call(s32[8,8,128]{2,1,0:T(8,128)} %get-tuple-element.9.places_ref, bf16[128,80,128]{2,1,0:T(8,128)(2,1)} %copy-done, bf16[8,8,2,128,128]{4,3,2,1,0:T(8,128)(2,1)} %get-tuple-element.11.blk_hbm), custom_call_target="tpu_custom_call" | custom-call | flops 335544320 | bytes 8552448 | tf_op jit(solution)/shard_map/pallas_call | solution.py:106
  148.3 0.0 copy-done.1
  148.3 1.6 %pad_maximum_fusion = bf16[8,128,128]{2,1,0:T(8,128)(2,1)} fusion(bf16[8,80,128]{2,1,0:T(8,128)(2,1)} %shard_map.49, bf16[8,48,128]{2,1,0:T(8,128)(2,1)S(1)} %copy-done.1), kind=kLoop, calls=%fused_computation | loop fusion | flops 524288 | bytes 524288 | tf_op jit(solution)/shard_map/concatenate | solution.py:163
Async XLA Ops:
  60.3 9.0 %copy-start.2 = (s32[8,2]{0,1:T(2,128)S(1)}, s32[8,2]{0,1:T(2,128)}, u32[]{:S(2)}) copy-start(s32[8,2]{0,1:T(2,128)} %param.6) | copy-start | bytes 196
  60.3 78.3 %all-to-all-start.1 = ((bf16[128,80,128]{2,1,0:T(8,128)(2,1)}), bf16[128,80,128]{2,1,0:T(8,128)(2,1)S(1)}, u32[]{:S(2)}, u32[]{:S(2)}) async-start(bf16[128,80,128]{2,1,0:T(8,128)(2,1)} %get-tuple-element.12), calls=%async_computation.1 | async-start | bytes 5242880 | tf_op jit(solution)/shard_map/all_to_all | solution.py:158
  128.1 20.1 %copy-start.1 = (bf16[8,48,128]{2,1,0:T(8,128)(2,1)S(1)}, bf16[8,48,128]{2,1,0:T(8,128)(2,1)}, u32[]{:S(2)}) copy-start(bf16[8,48,128]{2,1,0:T(8,128)(2,1)} %shard_map.48) | copy-start | bytes 294916
  138.7 1.5 %copy-start = (bf16[128,80,128]{2,1,0:T(8,128)(2,1)}, bf16[128,80,128]{2,1,0:T(8,128)(2,1)S(1)}, u32[]{:S(2)}) copy-start(bf16[128,80,128]{2,1,0:T(8,128)(2,1)S(1)} %all-to-all-done.1.recv_hbm) | copy-start | bytes 7864324

commit v11 on v8

--- a/solution.py
+++ b/solution.py
@@ -129,16 +129,14 @@
     )(places, head, tail, blocks)
 
 
-def pick_kernel(n_out, cut, sel_ref, amp_ref, head_hbm, tail_hbm, sems):
-    copies = []
-    for j in range(n_out):
-        src = amp_ref.at[sel_ref[j]]
-        copies.append(pltpu.make_async_copy(src.at[pl.ds(0, cut)], head_hbm.at[j], sems.at[0, j]))
-        copies.append(pltpu.make_async_copy(src.at[pl.ds(cut, src.shape[0] - cut)], tail_hbm.at[j], sems.at[1, j]))
-    for c in copies:
-        c.start()
-    for c in copies:
-        c.wait()
+def pick_kernel(n_out, cut, sel_ref, amp_ref, head_ref, tail_ref):
+    def body(j, carry):
+        tile = amp_ref[sel_ref[j]]
+        head_ref[j] = tile[:cut]
+        tail_ref[j] = tile[cut:]
+        return carry
+
+    lax.fori_loop(0, n_out, body, 0)
 
 
 def pick_outgoing(amplitudes, selection, cut):
@@ -150,8 +148,7 @@
             jax.ShapeDtypeStruct((n_out, rows - cut, t), amplitudes.dtype),
         ),
         in_specs=[pl.BlockSpec(memory_space=pltpu.SMEM), pl.BlockSpec(memory_space=pltpu.VMEM)],
-        out_specs=(pl.BlockSpec(memory_space=pl.ANY), pl.BlockSpec(memory_space=pl.ANY)),
-        scratch_shapes=[pltpu.SemaphoreType.DMA((2, n_out))],
+        out_specs=(pl.BlockSpec(memory_space=pltpu.VMEM), pl.BlockSpec(memory_space=pltpu.VMEM)),
         cost_estimate=pl.CostEstimate(flops=0, transcendentals=0, bytes_accessed=4 * n_out * amplitudes[0].size),
     )(selection, amplitudes)
 

time: 150 us -> 149 us (level)
  the two profiles are of different devices: /device:TPU:158 before, /device:TPU:152 now
where the time goes in v11:
time: 149 us; the launch traced here: 148 us
  Pallas kernels  63.7 us (43%)
  blocking collectives  55 us (37%)
  waiting for transfers between devices  18.4 us (12%)
  starting transfers between devices  8.98 us (6%)
  local copies, waits for them, and re-layouts  2.22 us (1%)
    all_to_all x1, blocking collectives, on_device(): head = lax.all_to_all(head, 'wide', split_axis=0, concat_axis=0, tiled=True)  55 us
    pallas_call x1, Pallas kernels, gather_integrals(): pl.pallas_call(functools.partial(gather_kernel, n_nar), out_shape=(jax.Sh...  50.3 us
    all_to_all x1, waiting for transfers between devices, on_device(): tail = lax.all_to_all(tail, 'wide', split_axis=0, concat_axis=0, tiled=True)  18.4 us
    pallas_call x1, Pallas kernels, ladder(): pl.pallas_call(functools.partial(ladder_kernel, n_x, n_k, per), out_shape...  9.39 us
    all_to_all x1, starting transfers between devices, on_device(): tail = lax.all_to_all(tail, 'wide', split_axis=0, concat_axis=0, tiled=True)  8.98 us
    pallas_call x1, Pallas kernels, pick_outgoing(): pl.pallas_call(functools.partial(pick_kernel, n_out, cut), out_shape=(jax...  4 us
  transfers between devices with their start and end apart: 1, of which 1 were waited for; matrix products, arithmetic and copies ran while one was open for 0% of the time, Pallas kernels for 34%

profile of v11, /device:TPU:152, one launch (start us, length us, event | category | flops | bytes accessed | tf_op | source)
XLA Modules:
  0.0 148.3 jit_solution(595574626659484560)
XLA Ops:
  0.0 4.0 %shard_map.47 = (bf16[128,48,128]{2,1,0:T(8,128)(2,1)}, bf16[128,80,128]{2,1,0:T(8,128)(2,1)}) custom-call(s32[128]{0:T(128)} %bitcast.1, bf16[16,128,128]{2,1,0:T(8,128)(2,1)} %amp_ref.1), custom_call_target="tpu_custom_call" | custom-call | bytes 8388608 | tf_op jit(solution)/shard_map/pallas_call | solution.py:144
  4.0 55.0 %all_to_all.10.head_hbm = bf16[128,48,128]{2,1,0:T(8,128)(2,1)} all-to-all(bf16[128,48,128]{2,1,0:T(8,128)(2,1)} %get-tuple-element.10), channel_id=1, replica_groups=mesh['wide'=64,'narrow'=8] {'wide'}, dimensions={0} | all-to-all | bytes 3145728 | tf_op jit(solution)/shard_map/all_to_all | solution.py:158
  59.0 0.0 copy-start.1
  59.0 9.0 %all-to-all-start.1 = ((bf16[128,80,128]{2,1,0:T(8,128)(2,1)}), bf16[128,80,128]{2,1,0:T(8,128)(2,1)S(1)}, u32[]{:S(2)}, u32[]{:S(2)}) async-start(bf16[128,80,128]{2,1,0:T(8,128)(2,1)} %get-tuple-element.11), calls=%async_computation.1 | async-start | bytes 5242880 | tf_op jit(solution)/shard_map/all_to_all | solution.py:159
  68.0 0.0 copy-done.1
  68.0 0.1 copy.5
  68.1 0.6 dynamic_update_slice.3.pos_ref
  68.7 50.3 %shard_map.46 = (bf16[8,8,2,128,128]{4,3,2,1,0:T(8,128)(2,1)}, s32[8,8,128]{2,1,0:T(8,128)}) custom-call(bf16[8,2,128,128]{3,2,1,0:T(8,128)(2,1)} %src_ref.1, s32[8,128]{1,0:T(8,128)} %dynamic_update_slice.3.pos_ref), custom_call_target="tpu_custom_call" | custom-call | bytes 8388608 | tf_op jit(solution)/shard_map/pallas_call | solution.py:58
  119.0 18.4 %all-to-all-done.1.tail_hbm = bf16[128,80,128]{2,1,0:T(8,128)(2,1)S(1)} async-done(((bf16[128,80,128]{2,1,0:T(8,128)(2,1)}), bf16[128,80,128]{2,1,0:T(8,128)(2,1)S(1)}, u32[]{:S(2)}, u32[]{:S(2)}) %all-to-all-start.1) | async-done | bytes 2621472 | tf_op jit(solution)/shard_map/all_to_all | solution.py:159
  137.4 0.0 copy-start
  137.4 1.5 %copy-done = bf16[128,80,128]{2,1,0:T(8,128)(2,1)} copy-done((bf16[128,80,128]{2,1,0:T(8,128)(2,1)}, bf16[128,80,128]{2,1,0:T(8,128)(2,1)S(1)}, u32[]{:S(2)}) %copy-start) | copy-done | bytes 2621464
  138.9 9.4 %shard_map.48 = bf16[8,128,128]{2,1,0:T(8,128)(2,1)} custom-call(s32[8,8,128]{2,1,0:T(8,128)} %get-tuple-element.9.places_ref, bf16[128,48,128]{2,1,0:T(8,128)(2,1)} %all_to_all.10.head_hbm, bf16[128,80,128]{2,1,0:T(8,128)(2,1)} %copy-done, bf16[8,8,2,128,128]{4,3,2,1,0:T(8,128)(2,1)} %get-tuple-element.12.blk_hbm), custom_call_target="tpu_custom_call" | custom-call | flops 536870912 | bytes 8650752 | tf_op jit(solution)/shard_map/pallas_call | solution.py:109
Async XLA Ops:
  59.0 9.0 %copy-start.1 = (s32[8,2]{0,1:T(2,128)S(1)}, s32[8,2]{0,1:T(2,128)}, u32[]{:S(2)}) copy-start(s32[8,2]{0,1:T(2,128)} %param.6) | copy-start | bytes 196
  59.0 78.3 %all-to-all-start.1 = ((bf16[128,80,128]{2,1,0:T(8,128)(2,1)}), bf16[128,80,128]{2,1,0:T(8,128)(2,1)S(1)}, u32[]{:S(2)}, u32[]{:S(2)}) async-start(bf16[128,80,128]{2,1,0:T(8,128)(2,1)} %get-tuple-element.11), calls=%async_computation.1 | async-start | bytes 5242880 | tf_op jit(solution)/shard_map/all_to_all | solution.py:159
  137.4 1.5 %copy-start = (bf16[128,80,128]{2,1,0:T(8,128)(2,1)}, bf16[128,80,128]{2,1,0:T(8,128)(2,1)S(1)}, u32[]{:S(2)}) copy-start(bf16[128,80,128]{2,1,0:T(8,128)(2,1)S(1)} %all-to-all-done.1.tail_hbm) | copy-start | bytes 7864324

commit v12 on v11

--- a/solution.py
+++ b/solution.py
@@ -76,30 +76,44 @@
 
 
 def ladder_kernel(n_x, n_k, per, places_ref, head_hbm, tail_hbm, blk_hbm, out_ref, tiles, blks, sems):
-    def copies(x, slot):
-        cut = head_hbm.shape[1]
-        picked = []
-        for k in range(n_k):
-            p = places_ref[k // per, x, k % per]
-            dst = tiles.at[slot, k]
-            picked.append(pltpu.make_async_copy(head_hbm.at[p], dst.at[pl.ds(0, cut)], sems.at[slot, 0, k]))
-            picked.append(
-                pltpu.make_async_copy(tail_hbm.at[p], dst.at[pl.ds(cut, dst.shape[0] - cut)], sems.at[slot, 1, k])
-            )
-        return picked + [pltpu.make_async_copy(blk_hbm.at[:, x], blks.at[slot], sems.at[slot, 2, 0])]
+    cut = head_hbm.shape[1]
 
+    def copies(pair, slot):
+        out = []
+        for sub in range(2):
+            x = 2 * pair + sub
+            for k in range(n_k):
+                p = places_ref[k // per, x, k % per]
+                dst = tiles.at[slot, sub, k]
+                out.append(pltpu.make_async_copy(head_hbm.at[p], dst.at[pl.ds(0, cut)], sems.at[slot, sub, 0, k]))
+                out.append(
+                    pltpu.make_async_copy(
+                        tail_hbm.at[p], dst.at[pl.ds(cut, dst.shape[0] - cut)], sems.at[slot, sub, 1, k]
+                    )
+                )
+            out.append(pltpu.make_async_copy(blk_hbm.at[:, x], blks.at[slot, sub], sems.at[slot, sub, 2, 0]))
+        return out
+
+    n_pairs = n_x // 2
     for c in copies(0, 0):
         c.start()
-    for x in range(n_x):
-        slot = x % 2
-        if x + 1 < n_x:
-            for c in copies(x + 1, 1 - slot):
+    for pair in range(n_pairs):
+        slot = pair % 2
+        if pair + 1 < n_pairs:
+            for c in copies(pair + 1, 1 - slot):
                 c.start()
-        for c in copies(x, slot):
+        for c in copies(pair, slot):
             c.wait()
-        lhs = jnp.concatenate([tiles[slot, k] for k in range(n_k)], axis=1)
-        rhs = blks[slot].reshape(n_k * blks.shape[-2], blks.shape[-1])
-        out_ref[x] = jnp.dot(lhs, rhs, preferred_element_type=jnp.float32).astype(out_ref.dtype)
+        lhs = jnp.concatenate(
+            [jnp.concatenate([tiles[slot, sub, k] for k in range(n_k)], axis=1) for sub in range(2)], axis=0
+        )
+        rhs = jnp.concatenate(
+            [blks[slot, sub].reshape(n_k * blks.shape[-2], blks.shape[-1]) for sub in range(2)], axis=1
+        )
+        res = jnp.dot(lhs, rhs, preferred_element_type=jnp.float32)
+        rows, cols = tiles.shape[-2], blks.shape[-1]
+        out_ref[2 * pair] = res[:rows, :cols].astype(out_ref.dtype)
+        out_ref[2 * pair + 1] = res[rows:, cols:].astype(out_ref.dtype)
 
 
 def ladder(places, head, tail, blocks):
@@ -117,9 +131,9 @@
         ],
         out_specs=pl.BlockSpec(memory_space=pltpu.VMEM),
         scratch_shapes=[
-            pltpu.VMEM((2, n_k, rows, t), head.dtype),
-            pltpu.VMEM((2, n_nar, per, t, s), blocks.dtype),
-            pltpu.SemaphoreType.DMA((2, 3, n_k)),
+            pltpu.VMEM((2, 2, n_k, rows, t), head.dtype),
+            pltpu.VMEM((2, 2, n_nar, per, t, s), blocks.dtype),
+            pltpu.SemaphoreType.DMA((2, 2, 3, n_k)),
         ],
         cost_estimate=pl.CostEstimate(
             flops=2 * n_x * n_k * rows * t * s,

time: 149 us -> 149 us (level)
  the two profiles are of different devices: /device:TPU:152 before, /device:TPU:110 now
where the time goes in v12:
time: 149 us; the launch traced here: 148 us
  Pallas kernels  61.9 us (42%)
  blocking collectives  55.8 us (37%)
  waiting for transfers between devices  19.2 us (13%)
  starting transfers between devices  8.98 us (6%)
  local copies, waits for them, and re-layouts  2.22 us (1%)
    all_to_all x1, blocking collectives, on_device(): head = lax.all_to_all(head, 'wide', split_axis=0, concat_axis=0, tiled=True)  55.8 us
    pallas_call x1, Pallas kernels, gather_integrals(): pl.pallas_call(functools.partial(gather_kernel, n_nar), out_shape=(jax.Sh...  48.7 us
    all_to_all x1, waiting for transfers between devices, on_device(): tail = lax.all_to_all(tail, 'wide', split_axis=0, concat_axis=0, tiled=True)  19.2 us
    pallas_call x1, Pallas kernels, ladder(): pl.pallas_call(functools.partial(ladder_kernel, n_x, n_k, per), out_shape...  9.19 us
    all_to_all x1, starting transfers between devices, on_device(): tail = lax.all_to_all(tail, 'wide', split_axis=0, concat_axis=0, tiled=True)  8.98 us
    pallas_call x1, Pallas kernels, pick_outgoing(): pl.pallas_call(functools.partial(pick_kernel, n_out, cut), out_shape=(jax...  4 us
  transfers between devices with their start and end apart: 1, of which 1 were waited for; matrix products, arithmetic and copies ran while one was open for 0% of the time, Pallas kernels for 33%

profile of v12, /device:TPU:110, one launch (start us, length us, event | category | flops | bytes accessed | tf_op | source)
XLA Modules:
  0.0 148.1 jit_solution(11146653755361495334)
XLA Ops:
  0.0 4.0 %shard_map.47 = (bf16[128,48,128]{2,1,0:T(8,128)(2,1)}, bf16[128,80,128]{2,1,0:T(8,128)(2,1)}) custom-call(s32[128]{0:T(128)} %bitcast.1, bf16[16,128,128]{2,1,0:T(8,128)(2,1)} %amp_ref.1), custom_call_target="tpu_custom_call" | custom-call | bytes 8388608 | tf_op jit(solution)/shard_map/pallas_call | solution.py:158
  4.0 55.8 %all_to_all.10.head_hbm = bf16[128,48,128]{2,1,0:T(8,128)(2,1)} all-to-all(bf16[128,48,128]{2,1,0:T(8,128)(2,1)} %get-tuple-element.10), channel_id=1, replica_groups=mesh['wide'=64,'narrow'=8] {'wide'}, dimensions={0} | all-to-all | bytes 3145728 | tf_op jit(solution)/shard_map/all_to_all | solution.py:172
  59.8 0.0 copy-start.1
  59.8 9.0 %all-to-all-start.1 = ((bf16[128,80,128]{2,1,0:T(8,128)(2,1)}), bf16[128,80,128]{2,1,0:T(8,128)(2,1)S(1)}, u32[]{:S(2)}, u32[]{:S(2)}) async-start(bf16[128,80,128]{2,1,0:T(8,128)(2,1)} %get-tuple-element.11), calls=%async_computation.1 | async-start | bytes 5242880 | tf_op jit(solution)/shard_map/all_to_all | solution.py:173
  68.8 0.0 copy-done.1
  68.8 0.1 copy.5
  68.9 0.6 dynamic_update_slice.3.pos_ref
  69.5 48.7 %shard_map.46 = (bf16[8,8,2,128,128]{4,3,2,1,0:T(8,128)(2,1)}, s32[8,8,128]{2,1,0:T(8,128)}) custom-call(bf16[8,2,128,128]{3,2,1,0:T(8,128)(2,1)} %src_ref.1, s32[8,128]{1,0:T(8,128)} %dynamic_update_slice.3.pos_ref), custom_call_target="tpu_custom_call" | custom-call | bytes 8388608 | tf_op jit(solution)/shard_map/pallas_call | solution.py:58
  118.2 19.2 %all-to-all-done.1.tail_hbm = bf16[128,80,128]{2,1,0:T(8,128)(2,1)S(1)} async-done(((bf16[128,80,128]{2,1,0:T(8,128)(2,1)}), bf16[128,80,128]{2,1,0:T(8,128)(2,1)S(1)}, u32[]{:S(2)}, u32[]{:S(2)}) %all-to-all-start.1) | async-done | bytes 2621472 | tf_op jit(solution)/shard_map/all_to_all | solution.py:173
  137.4 0.0 copy-start
  137.4 1.5 %copy-done = bf16[128,80,128]{2,1,0:T(8,128)(2,1)} copy-done((bf16[128,80,128]{2,1,0:T(8,128)(2,1)}, bf16[128,80,128]{2,1,0:T(8,128)(2,1)S(1)}, u32[]{:S(2)}) %copy-start) | copy-done | bytes 2621464
  138.9 9.2 %shard_map.48 = bf16[8,128,128]{2,1,0:T(8,128)(2,1)} custom-call(s32[8,8,128]{2,1,0:T(8,128)} %get-tuple-element.9.places_ref, bf16[128,48,128]{2,1,0:T(8,128)(2,1)} %all_to_all.10.head_hbm, bf16[128,80,128]{2,1,0:T(8,128)(2,1)} %copy-done, bf16[8,8,2,128,128]{4,3,2,1,0:T(8,128)(2,1)} %get-tuple-element.12.blk_hbm), custom_call_target="tpu_custom_call" | custom-call | flops 536870912 | bytes 8650752 | tf_op jit(solution)/shard_map/pallas_call | solution.py:123
Async XLA Ops:
  59.8 9.0 %copy-start.1 = (s32[8,2]{0,1:T(2,128)S(1)}, s32[8,2]{0,1:T(2,128)}, u32[]{:S(2)}) copy-start(s32[8,2]{0,1:T(2,128)} %param.6) | copy-start | bytes 196
  59.8 77.5 %all-to-all-start.1 = ((bf16[128,80,128]{2,1,0:T(8,128)(2,1)}), bf16[128,80,128]{2,1,0:T(8,128)(2,1)S(1)}, u32[]{:S(2)}, u32[]{:S(2)}) async-start(bf16[128,80,128]{2,1,0:T(8,128)(2,1)} %get-tuple-element.11), calls=%async_computation.1 | async-start | bytes 5242880 | tf_op jit(solution)/shard_map/all_to_all | solution.py:173
  137.4 1.5 %copy-start = (bf16[128,80,128]{2,1,0:T(8,128)(2,1)}, bf16[128,80,128]{2,1,0:T(8,128)(2,1)S(1)}, u32[]{:S(2)}) copy-start(bf16[128,80,128]{2,1,0:T(8,128)(2,1)S(1)} %all-to-all-done.1.tail_hbm) | copy-start | bytes 7864324

commit v13 on v11

--- a/solution.py
+++ b/solution.py
@@ -75,29 +75,30 @@
     )(integrals, positions)
 
 
-def ladder_kernel(n_x, n_k, per, places_ref, head_hbm, tail_hbm, blk_hbm, out_ref, tiles, blks, sems):
-    def copies(x, slot):
-        cut = head_hbm.shape[1]
+def ladder_kernel(n_x, n_k, per, places_ref, head_hbm, tail_hbm, blk_hbm, out_ref, head_v, tail_v, blks, sems):
+    whole = [
+        pltpu.make_async_copy(head_hbm, head_v, sems.at[0]),
+        pltpu.make_async_copy(tail_hbm, tail_v, sems.at[1]),
+    ]
+
+    def blk_copy(x, slot):
+        return pltpu.make_async_copy(blk_hbm.at[:, x], blks.at[slot], sems.at[2 + slot])
+
+    for c in whole:
+        c.start()
+    blk_copy(0, 0).start()
+    for c in whole:
+        c.wait()
+    for x in range(n_x):
+        slot = x % 2
+        if x + 1 < n_x:
+            blk_copy(x + 1, 1 - slot).start()
+        blk_copy(x, slot).wait()
         picked = []
         for k in range(n_k):
             p = places_ref[k // per, x, k % per]
-            dst = tiles.at[slot, k]
-            picked.append(pltpu.make_async_copy(head_hbm.at[p], dst.at[pl.ds(0, cut)], sems.at[slot, 0, k]))
-            picked.append(
-                pltpu.make_async_copy(tail_hbm.at[p], dst.at[pl.ds(cut, dst.shape[0] - cut)], sems.at[slot, 1, k])
-            )
-        return picked + [pltpu.make_async_copy(blk_hbm.at[:, x], blks.at[slot], sems.at[slot, 2, 0])]
-
-    for c in copies(0, 0):
-        c.start()
-    for x in range(n_x):
-        slot = x % 2
-        if x + 1 < n_x:
-            for c in copies(x + 1, 1 - slot):
-                c.start()
-        for c in copies(x, slot):
-            c.wait()
-        lhs = jnp.concatenate([tiles[slot, k] for k in range(n_k)], axis=1)
+            picked.append(jnp.concatenate([head_v[p], tail_v[p]], axis=0))
+        lhs = jnp.concatenate(picked, axis=1)
         rhs = blks[slot].reshape(n_k * blks.shape[-2], blks.shape[-1])
         out_ref[x] = jnp.dot(lhs, rhs, preferred_element_type=jnp.float32).astype(out_ref.dtype)
 
@@ -117,9 +118,10 @@
         ],
         out_specs=pl.BlockSpec(memory_space=pltpu.VMEM),
         scratch_shapes=[
-            pltpu.VMEM((2, n_k, rows, t), head.dtype),
+            pltpu.VMEM(head.shape, head.dtype),
+            pltpu.VMEM(tail.shape, tail.dtype),
             pltpu.VMEM((2, n_nar, per, t, s), blocks.dtype),
-            pltpu.SemaphoreType.DMA((2, 3, n_k)),
+            pltpu.SemaphoreType.DMA((4,)),
         ],
         cost_estimate=pl.CostEstimate(
             flops=2 * n_x * n_k * rows * t * s,

time: 149 us -> 149 us (level)
  the two profiles are of different devices: /device:TPU:152 before, /device:TPU:158 now
where the time goes in v13:
time: 149 us; the launch traced here: 148 us
  Pallas kernels  61.7 us (41%)
  blocking collectives  55 us (37%)
  waiting for transfers between devices  20 us (13%)
  starting transfers between devices  8.98 us (6%)
  local copies, waits for them, and re-layouts  2.22 us (1%)
    all_to_all x1, blocking collectives, on_device(): head = lax.all_to_all(head, 'wide', split_axis=0, concat_axis=0, tiled=True)  55 us
    pallas_call x1, Pallas kernels, gather_integrals(): pl.pallas_call(functools.partial(gather_kernel, n_nar), out_shape=(jax.Sh...  48.7 us
    all_to_all x1, waiting for transfers between devices, on_device(): tail = lax.all_to_all(tail, 'wide', split_axis=0, concat_axis=0, tiled=True)  20 us
    pallas_call x1, Pallas kernels, ladder(): pl.pallas_call(functools.partial(ladder_kernel, n_x, n_k, per), out_shape...  9.07 us
    all_to_all x1, starting transfers between devices, on_device(): tail = lax.all_to_all(tail, 'wide', split_axis=0, concat_axis=0, tiled=True)  8.98 us
    pallas_call x1, Pallas kernels, pick_outgoing(): pl.pallas_call(functools.partial(pick_kernel, n_out, cut), out_shape=(jax...  4 us
  transfers between devices with their start and end apart: 1, of which 1 were waited for; matrix products, arithmetic and copies ran while one was open for 0% of the time, Pallas kernels for 33%

profile of v13, /device:TPU:158, one launch (start us, length us, event | category | flops | bytes accessed | tf_op | source)
XLA Modules:
  0.0 148.0 jit_solution(10133127926261241659)
XLA Ops:
  0.0 4.0 %shard_map.47 = (bf16[128,48,128]{2,1,0:T(8,128)(2,1)}, bf16[128,80,128]{2,1,0:T(8,128)(2,1)}) custom-call(s32[128]{0:T(128)} %bitcast.1, bf16[16,128,128]{2,1,0:T(8,128)(2,1)} %amp_ref.1), custom_call_target="tpu_custom_call" | custom-call | bytes 8388608 | tf_op jit(solution)/shard_map/pallas_call | solution.py:146
  4.0 55.0 %all_to_all.10.head_hbm = bf16[128,48,128]{2,1,0:T(8,128)(2,1)} all-to-all(bf16[128,48,128]{2,1,0:T(8,128)(2,1)} %get-tuple-element.10), channel_id=1, replica_groups=mesh['wide'=64,'narrow'=8] {'wide'}, dimensions={0} | all-to-all | bytes 3145728 | tf_op jit(solution)/shard_map/all_to_all | solution.py:160
  59.0 0.0 copy-start.1
  59.0 9.0 %all-to-all-start.1 = ((bf16[128,80,128]{2,1,0:T(8,128)(2,1)}), bf16[128,80,128]{2,1,0:T(8,128)(2,1)S(1)}, u32[]{:S(2)}, u32[]{:S(2)}) async-start(bf16[128,80,128]{2,1,0:T(8,128)(2,1)} %get-tuple-element.11), calls=%async_computation.1 | async-start | bytes 5242880 | tf_op jit(solution)/shard_map/all_to_all | solution.py:161
  68.0 0.0 copy-done.1
  68.0 0.1 copy.5
  68.1 0.6 dynamic_update_slice.3.pos_ref
  68.7 48.7 %shard_map.46 = (bf16[8,8,2,128,128]{4,3,2,1,0:T(8,128)(2,1)}, s32[8,8,128]{2,1,0:T(8,128)}) custom-call(bf16[8,2,128,128]{3,2,1,0:T(8,128)(2,1)} %src_ref.1, s32[8,128]{1,0:T(8,128)} %dynamic_update_slice.3.pos_ref), custom_call_target="tpu_custom_call" | custom-call | bytes 8388608 | tf_op jit(solution)/shard_map/pallas_call | solution.py:58
  117.4 20.0 %all-to-all-done.1.tail_hbm = bf16[128,80,128]{2,1,0:T(8,128)(2,1)S(1)} async-done(((bf16[128,80,128]{2,1,0:T(8,128)(2,1)}), bf16[128,80,128]{2,1,0:T(8,128)(2,1)S(1)}, u32[]{:S(2)}, u32[]{:S(2)}) %all-to-all-start.1) | async-done | bytes 2621472 | tf_op jit(solution)/shard_map/all_to_all | solution.py:161
  137.4 0.0 copy-start
  137.4 1.5 %copy-done = bf16[128,80,128]{2,1,0:T(8,128)(2,1)} copy-done((bf16[128,80,128]{2,1,0:T(8,128)(2,1)}, bf16[128,80,128]{2,1,0:T(8,128)(2,1)S(1)}, u32[]{:S(2)}) %copy-start) | copy-done | bytes 2621464
  138.9 9.1 %shard_map.48 = bf16[8,128,128]{2,1,0:T(8,128)(2,1)} custom-call(s32[8,8,128]{2,1,0:T(8,128)} %get-tuple-element.9.places_ref, bf16[128,48,128]{2,1,0:T(8,128)(2,1)} %all_to_all.10.head_hbm, bf16[128,80,128]{2,1,0:T(8,128)(2,1)} %copy-done, bf16[8,8,2,128,128]{4,3,2,1,0:T(8,128)(2,1)} %get-tuple-element.12.blk_hbm), custom_call_target="tpu_custom_call" | custom-call | flops 536870912 | bytes 8650752 | tf_op jit(solution)/shard_map/pallas_call | solution.py:110
Async XLA Ops:
  59.0 9.0 %copy-start.1 = (s32[8,2]{0,1:T(2,128)S(1)}, s32[8,2]{0,1:T(2,128)}, u32[]{:S(2)}) copy-start(s32[8,2]{0,1:T(2,128)} %param.6) | copy-start | bytes 196
  59.0 78.3 %all-to-all-start.1 = ((bf16[128,80,128]{2,1,0:T(8,128)(2,1)}), bf16[128,80,128]{2,1,0:T(8,128)(2,1)S(1)}, u32[]{:S(2)}, u32[]{:S(2)}) async-start(bf16[128,80,128]{2,1,0:T(8,128)(2,1)} %get-tuple-element.11), calls=%async_computation.1 | async-start | bytes 5242880 | tf_op jit(solution)/shard_map/all_to_all | solution.py:161
  137.4 1.5 %copy-start = (bf16[128,80,128]{2,1,0:T(8,128)(2,1)}, bf16[128,80,128]{2,1,0:T(8,128)(2,1)S(1)}, u32[]{:S(2)}) copy-start(bf16[128,80,128]{2,1,0:T(8,128)(2,1)S(1)} %all-to-all-done.1.tail_hbm) | copy-start | bytes 7864324

commit v14 on v13

--- a/solution.py
+++ b/solution.py
@@ -75,31 +75,23 @@
     )(integrals, positions)
 
 
-def ladder_kernel(n_x, n_k, per, places_ref, head_hbm, tail_hbm, blk_hbm, out_ref, head_v, tail_v, blks, sems):
+def ladder_kernel(n_x, n_k, per, places_ref, head_hbm, tail_hbm, blk_hbm, out_ref, head_v, tail_v, blk_v, sems):
     whole = [
         pltpu.make_async_copy(head_hbm, head_v, sems.at[0]),
         pltpu.make_async_copy(tail_hbm, tail_v, sems.at[1]),
+        pltpu.make_async_copy(blk_hbm, blk_v, sems.at[2]),
     ]
-
-    def blk_copy(x, slot):
-        return pltpu.make_async_copy(blk_hbm.at[:, x], blks.at[slot], sems.at[2 + slot])
-
     for c in whole:
         c.start()
-    blk_copy(0, 0).start()
     for c in whole:
         c.wait()
     for x in range(n_x):
-        slot = x % 2
-        if x + 1 < n_x:
-            blk_copy(x + 1, 1 - slot).start()
-        blk_copy(x, slot).wait()
         picked = []
         for k in range(n_k):
             p = places_ref[k // per, x, k % per]
             picked.append(jnp.concatenate([head_v[p], tail_v[p]], axis=0))
         lhs = jnp.concatenate(picked, axis=1)
-        rhs = blks[slot].reshape(n_k * blks.shape[-2], blks.shape[-1])
+        rhs = blk_v[:, x].reshape(n_k * blk_v.shape[-2], blk_v.shape[-1])
         out_ref[x] = jnp.dot(lhs, rhs, preferred_element_type=jnp.float32).astype(out_ref.dtype)
 
 
@@ -120,8 +112,8 @@
         scratch_shapes=[
             pltpu.VMEM(head.shape, head.dtype),
             pltpu.VMEM(tail.shape, tail.dtype),
-            pltpu.VMEM((2, n_nar, per, t, s), blocks.dtype),
-            pltpu.SemaphoreType.DMA((4,)),
+            pltpu.VMEM(blocks.shape, blocks.dtype),
+            pltpu.SemaphoreType.DMA((3,)),
         ],
         cost_estimate=pl.CostEstimate(
             flops=2 * n_x * n_k * rows * t * s,

time: 149 us -> 146 us (0.980)
  the two profiles are of different devices: /device:TPU:158 before, /device:TPU:156 now
where the time goes in v14:
time: 146 us
  Pallas kernels  59.2 us (41%)
  blocking collectives  55 us (38%)
  waiting for transfers between devices  20.1 us (14%)
  starting transfers between devices  8.98 us (6%)
  local copies, waits for them, and re-layouts  2.22 us (2%)
    all_to_all x1, blocking collectives, on_device(): head = lax.all_to_all(head, 'wide', split_axis=0, concat_axis=0, tiled=True)  55 us
    pallas_call x1, Pallas kernels, gather_integrals(): pl.pallas_call(functools.partial(gather_kernel, n_nar), out_shape=(jax.Sh...  48.5 us
    all_to_all x1, waiting for transfers between devices, on_device(): tail = lax.all_to_all(tail, 'wide', split_axis=0, concat_axis=0, tiled=True)  20.1 us
    all_to_all x1, starting transfers between devices, on_device(): tail = lax.all_to_all(tail, 'wide', split_axis=0, concat_axis=0, tiled=True)  8.98 us
    pallas_call x1, Pallas kernels, ladder(): pl.pallas_call(functools.partial(ladder_kernel, n_x, n_k, per), out_shape...  6.69 us
    pallas_call x1, Pallas kernels, pick_outgoing(): pl.pallas_call(functools.partial(pick_kernel, n_out, cut), out_shape=(jax...  4 us
  transfers between devices with their start and end apart: 1, of which 1 were waited for; matrix products, arithmetic and copies ran while one was open for 0% of the time, Pallas kernels for 33%

profile of v14, /device:TPU:156, one launch (start us, length us, event | category | flops | bytes accessed | tf_op | source)
XLA Modules:
  0.0 145.6 jit_solution(15005713705060540507)
XLA Ops:
  0.0 4.0 %shard_map.47 = (bf16[128,48,128]{2,1,0:T(8,128)(2,1)}, bf16[128,80,128]{2,1,0:T(8,128)(2,1)}) custom-call(s32[128]{0:T(128)} %bitcast.1, bf16[16,128,128]{2,1,0:T(8,128)(2,1)} %amp_ref.1), custom_call_target="tpu_custom_call" | custom-call | bytes 8388608 | tf_op jit(solution)/shard_map/pallas_call | solution.py:138
  4.0 55.0 %all_to_all.10.head_hbm = bf16[128,48,128]{2,1,0:T(8,128)(2,1)} all-to-all(bf16[128,48,128]{2,1,0:T(8,128)(2,1)} %get-tuple-element.10), channel_id=1, replica_groups=mesh['wide'=64,'narrow'=8] {'wide'}, dimensions={0} | all-to-all | bytes 3145728 | tf_op jit(solution)/shard_map/all_to_all | solution.py:152
  59.0 0.0 copy-start.1
  59.0 9.0 %all-to-all-start.1 = ((bf16[128,80,128]{2,1,0:T(8,128)(2,1)}), bf16[128,80,128]{2,1,0:T(8,128)(2,1)S(1)}, u32[]{:S(2)}, u32[]{:S(2)}) async-start(bf16[128,80,128]{2,1,0:T(8,128)(2,1)} %get-tuple-element.11), calls=%async_computation.1 | async-start | bytes 5242880 | tf_op jit(solution)/shard_map/all_to_all | solution.py:153
  68.0 0.0 copy-done.1
  68.0 0.1 copy.5
  68.1 0.6 dynamic_update_slice.3.pos_ref
  68.7 48.5 %shard_map.46 = (bf16[8,8,2,128,128]{4,3,2,1,0:T(8,128)(2,1)}, s32[8,8,128]{2,1,0:T(8,128)}) custom-call(bf16[8,2,128,128]{3,2,1,0:T(8,128)(2,1)} %src_ref.1, s32[8,128]{1,0:T(8,128)} %dynamic_update_slice.3.pos_ref), custom_call_target="tpu_custom_call" | custom-call | bytes 8388608 | tf_op jit(solution)/shard_map/pallas_call | solution.py:58
  117.2 20.1 %all-to-all-done.1.tail_hbm = bf16[128,80,128]{2,1,0:T(8,128)(2,1)S(1)} async-done(((bf16[128,80,128]{2,1,0:T(8,128)(2,1)}), bf16[128,80,128]{2,1,0:T(8,128)(2,1)S(1)}, u32[]{:S(2)}, u32[]{:S(2)}) %all-to-all-start.1) | async-done | bytes 2621472 | tf_op jit(solution)/shard_map/all_to_all | solution.py:153
  137.4 0.0 copy-start
  137.4 1.5 %copy-done = bf16[128,80,128]{2,1,0:T(8,128)(2,1)} copy-done((bf16[128,80,128]{2,1,0:T(8,128)(2,1)}, bf16[128,80,128]{2,1,0:T(8,128)(2,1)S(1)}, u32[]{:S(2)}) %copy-start) | copy-done | bytes 2621464
  138.9 6.7 %shard_map.48 = bf16[8,128,128]{2,1,0:T(8,128)(2,1)} custom-call(s32[8,8,128]{2,1,0:T(8,128)} %get-tuple-element.9.places_ref, bf16[128,48,128]{2,1,0:T(8,128)(2,1)} %all_to_all.10.head_hbm, bf16[128,80,128]{2,1,0:T(8,128)(2,1)} %copy-done, bf16[8,8,2,128,128]{4,3,2,1,0:T(8,128)(2,1)} %get-tuple-element.12.blk_hbm), custom_call_target="tpu_custom_call" | custom-call | flops 536870912 | bytes 8650752 | tf_op jit(solution)/shard_map/pallas_call | solution.py:102
Async XLA Ops:
  59.0 9.0 %copy-start.1 = (s32[8,2]{0,1:T(2,128)S(1)}, s32[8,2]{0,1:T(2,128)}, u32[]{:S(2)}) copy-start(s32[8,2]{0,1:T(2,128)} %param.6) | copy-start | bytes 196
  59.0 78.3 %all-to-all-start.1 = ((bf16[128,80,128]{2,1,0:T(8,128)(2,1)}), bf16[128,80,128]{2,1,0:T(8,128)(2,1)S(1)}, u32[]{:S(2)}, u32[]{:S(2)}) async-start(bf16[128,80,128]{2,1,0:T(8,128)(2,1)} %get-tuple-element.11), calls=%async_computation.1 | async-start | bytes 5242880 | tf_op jit(solution)/shard_map/all_to_all | solution.py:153
  137.4 1.5 %copy-start = (bf16[128,80,128]{2,1,0:T(8,128)(2,1)}, bf16[128,80,128]{2,1,0:T(8,128)(2,1)S(1)}, u32[]{:S(2)}) copy-start(bf16[128,80,128]{2,1,0:T(8,128)(2,1)S(1)} %all-to-all-done.1.tail_hbm) | copy-start | bytes 7864324

commit v15 on v14

--- a/solution.py
+++ b/solution.py
@@ -75,24 +75,33 @@
     )(integrals, positions)
 
 
-def ladder_kernel(n_x, n_k, per, places_ref, head_hbm, tail_hbm, blk_hbm, out_ref, head_v, tail_v, blk_v, sems):
-    whole = [
+def ladder_kernel(n_x, n_k, per, places_ref, head_hbm, tail_hbm, blk_hbm, out_ref, head_v, tail_v, blk_v, acc, sems):
+    half = blk_v.shape[0] // 2
+    parts = (pl.ds(0, half), pl.ds(half, blk_v.shape[0] - half))
+    copies = [
         pltpu.make_async_copy(head_hbm, head_v, sems.at[0]),
         pltpu.make_async_copy(tail_hbm, tail_v, sems.at[1]),
-        pltpu.make_async_copy(blk_hbm, blk_v, sems.at[2]),
-    ]
-    for c in whole:
+    ] + [pltpu.make_async_copy(blk_hbm.at[r], blk_v.at[r], sems.at[2 + i]) for i, r in enumerate(parts)]
+    for c in copies:
         c.start()
-    for c in whole:
+    for c in copies[:3]:
         c.wait()
-    for x in range(n_x):
-        picked = []
-        for k in range(n_k):
-            p = places_ref[k // per, x, k % per]
-            picked.append(jnp.concatenate([head_v[p], tail_v[p]], axis=0))
-        lhs = jnp.concatenate(picked, axis=1)
-        rhs = blk_v[:, x].reshape(n_k * blk_v.shape[-2], blk_v.shape[-1])
-        out_ref[x] = jnp.dot(lhs, rhs, preferred_element_type=jnp.float32).astype(out_ref.dtype)
+    for h, r in enumerate(parts):
+        if h == 1:
+            copies[3].wait()
+        ks = range(h * half * per, (h * half + r.size) * per)
+        for x in range(n_x):
+            picked = []
+            for k in ks:
+                p = places_ref[k // per, x, k % per]
+                picked.append(jnp.concatenate([head_v[p], tail_v[p]], axis=0))
+            lhs = jnp.concatenate(picked, axis=1)
+            rhs = blk_v[r, x].reshape(len(ks) * blk_v.shape[-2], blk_v.shape[-1])
+            part = jnp.dot(lhs, rhs, preferred_element_type=jnp.float32)
+            if h == 0:
+                acc[x] = part
+            else:
+                out_ref[x] = (acc[x] + part).astype(out_ref.dtype)
 
 
 def ladder(places, head, tail, blocks):
@@ -113,7 +122,8 @@
             pltpu.VMEM(head.shape, head.dtype),
             pltpu.VMEM(tail.shape, tail.dtype),
             pltpu.VMEM(blocks.shape, blocks.dtype),
-            pltpu.SemaphoreType.DMA((3,)),
+            pltpu.VMEM((n_x, rows, s), jnp.float32),
+            pltpu.SemaphoreType.DMA((4,)),
         ],
         cost_estimate=pl.CostEstimate(
             flops=2 * n_x * n_k * rows * t * s,

time: 146 us -> 146 us (level)
  the two profiles are of different devices: /device:TPU:156 before, /device:TPU:152 now
where the time goes in v15:
time: 146 us; the launch traced here: 145 us
  Pallas kernels  60.5 us (41%)
  blocking collectives  55 us (38%)
  waiting for transfers between devices  18.4 us (13%)
  starting transfers between devices  8.98 us (6%)
  local copies, waits for them, and re-layouts  2.22 us (2%)
    all_to_all x1, blocking collectives, on_device(): head = lax.all_to_all(head, 'wide', split_axis=0, concat_axis=0, tiled=True)  55 us
    pallas_call x1, Pallas kernels, gather_integrals(): pl.pallas_call(functools.partial(gather_kernel, n_nar), out_shape=(jax.Sh...  50.3 us
    all_to_all x1, waiting for transfers between devices, on_device(): tail = lax.all_to_all(tail, 'wide', split_axis=0, concat_axis=0, tiled=True)  18.4 us
    all_to_all x1, starting transfers between devices, on_device(): tail = lax.all_to_all(tail, 'wide', split_axis=0, concat_axis=0, tiled=True)  8.98 us
    pallas_call x1, Pallas kernels, ladder(): pl.pallas_call(functools.partial(ladder_kernel, n_x, n_k, per), out_shape...  6.26 us
    pallas_call x1, Pallas kernels, pick_outgoing(): pl.pallas_call(functools.partial(pick_kernel, n_out, cut), out_shape=(jax...  4 us
  transfers between devices with their start and end apart: 1, of which 1 were waited for; matrix products, arithmetic and copies ran while one was open for 0% of the time, Pallas kernels for 35%

profile of v15, /device:TPU:152, one launch (start us, length us, event | category | flops | bytes accessed | tf_op | source)
XLA Modules:
  0.0 145.2 jit_solution(319041636921190236)
XLA Ops:
  0.0 4.0 %shard_map.47 = (bf16[128,48,128]{2,1,0:T(8,128)(2,1)}, bf16[128,80,128]{2,1,0:T(8,128)(2,1)}) custom-call(s32[128]{0:T(128)} %bitcast.1, bf16[16,128,128]{2,1,0:T(8,128)(2,1)} %amp_ref.1), custom_call_target="tpu_custom_call" | custom-call | bytes 8388608 | tf_op jit(solution)/shard_map/pallas_call | solution.py:148
  4.0 55.0 %all_to_all.10.head_hbm = bf16[128,48,128]{2,1,0:T(8,128)(2,1)} all-to-all(bf16[128,48,128]{2,1,0:T(8,128)(2,1)} %get-tuple-element.10), channel_id=1, replica_groups=mesh['wide'=64,'narrow'=8] {'wide'}, dimensions={0} | all-to-all | bytes 3145728 | tf_op jit(solution)/shard_map/all_to_all | solution.py:162
  59.0 0.0 copy-start.1
  59.0 9.0 %all-to-all-start.1 = ((bf16[128,80,128]{2,1,0:T(8,128)(2,1)}), bf16[128,80,128]{2,1,0:T(8,128)(2,1)S(1)}, u32[]{:S(2)}, u32[]{:S(2)}) async-start(bf16[128,80,128]{2,1,0:T(8,128)(2,1)} %get-tuple-element.11), calls=%async_computation.1 | async-start | bytes 5242880 | tf_op jit(solution)/shard_map/all_to_all | solution.py:163
  68.0 0.0 copy-done.1
  68.0 0.1 copy.5
  68.1 0.6 dynamic_update_slice.3.pos_ref
  68.7 50.3 %shard_map.46 = (bf16[8,8,2,128,128]{4,3,2,1,0:T(8,128)(2,1)}, s32[8,8,128]{2,1,0:T(8,128)}) custom-call(bf16[8,2,128,128]{3,2,1,0:T(8,128)(2,1)} %src_ref.1, s32[8,128]{1,0:T(8,128)} %dynamic_update_slice.3.pos_ref), custom_call_target="tpu_custom_call" | custom-call | bytes 8388608 | tf_op jit(solution)/shard_map/pallas_call | solution.py:58
  119.0 18.4 %all-to-all-done.1.tail_hbm = bf16[128,80,128]{2,1,0:T(8,128)(2,1)S(1)} async-done(((bf16[128,80,128]{2,1,0:T(8,128)(2,1)}), bf16[128,80,128]{2,1,0:T(8,128)(2,1)S(1)}, u32[]{:S(2)}, u32[]{:S(2)}) %all-to-all-start.1) | async-done | bytes 2621472 | tf_op jit(solution)/shard_map/all_to_all | solution.py:163
  137.4 0.0 copy-start
  137.4 1.5 %copy-done = bf16[128,80,128]{2,1,0:T(8,128)(2,1)} copy-done((bf16[128,80,128]{2,1,0:T(8,128)(2,1)}, bf16[128,80,128]{2,1,0:T(8,128)(2,1)S(1)}, u32[]{:S(2)}) %copy-start) | copy-done | bytes 2621464
  138.9 6.3 %shard_map.48 = bf16[8,128,128]{2,1,0:T(8,128)(2,1)} custom-call(s32[8,8,128]{2,1,0:T(8,128)} %get-tuple-element.9.places_ref, bf16[128,48,128]{2,1,0:T(8,128)(2,1)} %all_to_all.10.head_hbm, bf16[128,80,128]{2,1,0:T(8,128)(2,1)} %copy-done, bf16[8,8,2,128,128]{4,3,2,1,0:T(8,128)(2,1)} %get-tuple-element.12.blk_hbm), custom_call_target="tpu_custom_call" | custom-call | flops 536870912 | bytes 8650752 | tf_op jit(solution)/shard_map/pallas_call | solution.py:111
Async XLA Ops:
  59.0 9.0 %copy-start.1 = (s32[8,2]{0,1:T(2,128)S(1)}, s32[8,2]{0,1:T(2,128)}, u32[]{:S(2)}) copy-start(s32[8,2]{0,1:T(2,128)} %param.6) | copy-start | bytes 196
  59.0 78.3 %all-to-all-start.1 = ((bf16[128,80,128]{2,1,0:T(8,128)(2,1)}), bf16[128,80,128]{2,1,0:T(8,128)(2,1)S(1)}, u32[]{:S(2)}, u32[]{:S(2)}) async-start(bf16[128,80,128]{2,1,0:T(8,128)(2,1)} %get-tuple-element.11), calls=%async_computation.1 | async-start | bytes 5242880 | tf_op jit(solution)/shard_map/all_to_all | solution.py:163
  137.4 1.5 %copy-start = (bf16[128,80,128]{2,1,0:T(8,128)(2,1)}, bf16[128,80,128]{2,1,0:T(8,128)(2,1)S(1)}, u32[]{:S(2)}) copy-start(bf16[128,80,128]{2,1,0:T(8,128)(2,1)S(1)} %all-to-all-done.1.tail_hbm) | copy-start | bytes 7864324

commit v16 on v15

--- a/solution.py
+++ b/solution.py
@@ -76,20 +76,20 @@
 
 
 def ladder_kernel(n_x, n_k, per, places_ref, head_hbm, tail_hbm, blk_hbm, out_ref, head_v, tail_v, blk_v, acc, sems):
-    half = blk_v.shape[0] // 2
-    parts = (pl.ds(0, half), pl.ds(half, blk_v.shape[0] - half))
+    n_parts = 4
+    step = blk_v.shape[0] // n_parts
+    parts = [pl.ds(i * step, step) for i in range(n_parts)]
     copies = [
         pltpu.make_async_copy(head_hbm, head_v, sems.at[0]),
         pltpu.make_async_copy(tail_hbm, tail_v, sems.at[1]),
     ] + [pltpu.make_async_copy(blk_hbm.at[r], blk_v.at[r], sems.at[2 + i]) for i, r in enumerate(parts)]
     for c in copies:
         c.start()
-    for c in copies[:3]:
-        c.wait()
+    copies[0].wait()
+    copies[1].wait()
     for h, r in enumerate(parts):
-        if h == 1:
-            copies[3].wait()
-        ks = range(h * half * per, (h * half + r.size) * per)
+        copies[2 + h].wait()
+        ks = range(h * step * per, (h + 1) * step * per)
         for x in range(n_x):
             picked = []
             for k in ks:
@@ -100,6 +100,8 @@
             part = jnp.dot(lhs, rhs, preferred_element_type=jnp.float32)
             if h == 0:
                 acc[x] = part
+            elif h < n_parts - 1:
+                acc[x] = acc[x] + part
             else:
                 out_ref[x] = (acc[x] + part).astype(out_ref.dtype)
 
@@ -123,7 +125,7 @@
             pltpu.VMEM(tail.shape, tail.dtype),
             pltpu.VMEM(blocks.shape, blocks.dtype),
             pltpu.VMEM((n_x, rows, s), jnp.float32),
-            pltpu.SemaphoreType.DMA((4,)),
+            pltpu.SemaphoreType.DMA((6,)),
         ],
         cost_estimate=pl.CostEstimate(
             flops=2 * n_x * n_k * rows * t * s,

time: 146 us -> 146 us (level)
  the two profiles are of different devices: /device:TPU:152 before, /device:TPU:154 now
where the time goes in v16:
time: 146 us; the launch traced here: 145 us
  Pallas kernels  59.6 us (41%)
  blocking collectives  55 us (38%)
  waiting for transfers between devices  19.3 us (13%)
  starting transfers between devices  8.98 us (6%)
  local copies, waits for them, and re-layouts  2.22 us (2%)
    all_to_all x1, blocking collectives, on_device(): head = lax.all_to_all(head, 'wide', split_axis=0, concat_axis=0, tiled=True)  55 us
    pallas_call x1, Pallas kernels, gather_integrals(): pl.pallas_call(functools.partial(gather_kernel, n_nar), out_shape=(jax.Sh...  49.4 us
    all_to_all x1, waiting for transfers between devices, on_device(): tail = lax.all_to_all(tail, 'wide', split_axis=0, concat_axis=0, tiled=True)  19.3 us
    all_to_all x1, starting transfers between devices, on_device(): tail = lax.all_to_all(tail, 'wide', split_axis=0, concat_axis=0, tiled=True)  8.98 us
    pallas_call x1, Pallas kernels, ladder(): pl.pallas_call(functools.partial(ladder_kernel, n_x, n_k, per), out_shape...  6.2 us
    pallas_call x1, Pallas kernels, pick_outgoing(): pl.pallas_call(functools.partial(pick_kernel, n_out, cut), out_shape=(jax...  4 us
  transfers between devices with their start and end apart: 1, of which 1 were waited for; matrix products, arithmetic and copies ran while one was open for 0% of the time, Pallas kernels for 34%

profile of v16, /device:TPU:154, one launch (start us, length us, event | category | flops | bytes accessed | tf_op | source)
XLA Modules:
  0.0 145.1 jit_solution(1236134219086552200)
XLA Ops:
  0.0 4.0 %shard_map.47 = (bf16[128,48,128]{2,1,0:T(8,128)(2,1)}, bf16[128,80,128]{2,1,0:T(8,128)(2,1)}) custom-call(s32[128]{0:T(128)} %bitcast.1, bf16[16,128,128]{2,1,0:T(8,128)(2,1)} %amp_ref.1), custom_call_target="tpu_custom_call" | custom-call | bytes 8388608 | tf_op jit(solution)/shard_map/pallas_call | solution.py:150
  4.0 55.0 %all_to_all.10.head_hbm = bf16[128,48,128]{2,1,0:T(8,128)(2,1)} all-to-all(bf16[128,48,128]{2,1,0:T(8,128)(2,1)} %get-tuple-element.10), channel_id=1, replica_groups=mesh['wide'=64,'narrow'=8] {'wide'}, dimensions={0} | all-to-all | bytes 3145728 | tf_op jit(solution)/shard_map/all_to_all | solution.py:164
  59.0 0.0 copy-start.1
  59.0 9.0 %all-to-all-start.1 = ((bf16[128,80,128]{2,1,0:T(8,128)(2,1)}), bf16[128,80,128]{2,1,0:T(8,128)(2,1)S(1)}, u32[]{:S(2)}, u32[]{:S(2)}) async-start(bf16[128,80,128]{2,1,0:T(8,128)(2,1)} %get-tuple-element.11), calls=%async_computation.1 | async-start | bytes 5242880 | tf_op jit(solution)/shard_map/all_to_all | solution.py:165
  68.0 0.0 copy-done.1
  68.0 0.1 copy.5
  68.1 0.6 dynamic_update_slice.3.pos_ref
  68.7 49.4 %shard_map.46 = (bf16[8,8,2,128,128]{4,3,2,1,0:T(8,128)(2,1)}, s32[8,8,128]{2,1,0:T(8,128)}) custom-call(bf16[8,2,128,128]{3,2,1,0:T(8,128)(2,1)} %src_ref.1, s32[8,128]{1,0:T(8,128)} %dynamic_update_slice.3.pos_ref), custom_call_target="tpu_custom_call" | custom-call | bytes 8388608 | tf_op jit(solution)/shard_map/pallas_call | solution.py:58
  118.1 19.3 %all-to-all-done.1.tail_hbm = bf16[128,80,128]{2,1,0:T(8,128)(2,1)S(1)} async-done(((bf16[128,80,128]{2,1,0:T(8,128)(2,1)}), bf16[128,80,128]{2,1,0:T(8,128)(2,1)S(1)}, u32[]{:S(2)}, u32[]{:S(2)}) %all-to-all-start.1) | async-done | bytes 2621472 | tf_op jit(solution)/shard_map/all_to_all | solution.py:165
  137.4 0.0 copy-start
  137.4 1.5 %copy-done = bf16[128,80,128]{2,1,0:T(8,128)(2,1)} copy-done((bf16[128,80,128]{2,1,0:T(8,128)(2,1)}, bf16[128,80,128]{2,1,0:T(8,128)(2,1)S(1)}, u32[]{:S(2)}) %copy-start) | copy-done | bytes 2621464
  138.9 6.2 %shard_map.48 = bf16[8,128,128]{2,1,0:T(8,128)(2,1)} custom-call(s32[8,8,128]{2,1,0:T(8,128)} %get-tuple-element.9.places_ref, bf16[128,48,128]{2,1,0:T(8,128)(2,1)} %all_to_all.10.head_hbm, bf16[128,80,128]{2,1,0:T(8,128)(2,1)} %copy-done, bf16[8,8,2,128,128]{4,3,2,1,0:T(8,128)(2,1)} %get-tuple-element.12.blk_hbm), custom_call_target="tpu_custom_call" | custom-call | flops 536870912 | bytes 8650752 | tf_op jit(solution)/shard_map/pallas_call | solution.py:113
Async XLA Ops:
  59.0 9.0 %copy-start.1 = (s32[8,2]{0,1:T(2,128)S(1)}, s32[8,2]{0,1:T(2,128)}, u32[]{:S(2)}) copy-start(s32[8,2]{0,1:T(2,128)} %param.6) | copy-start | bytes 196
  59.0 78.3 %all-to-all-start.1 = ((bf16[128,80,128]{2,1,0:T(8,128)(2,1)}), bf16[128,80,128]{2,1,0:T(8,128)(2,1)S(1)}, u32[]{:S(2)}, u32[]{:S(2)}) async-start(bf16[128,80,128]{2,1,0:T(8,128)(2,1)} %get-tuple-element.11), calls=%async_computation.1 | async-start | bytes 5242880 | tf_op jit(solution)/shard_map/all_to_all | solution.py:165
  137.4 1.5 %copy-start = (bf16[128,80,128]{2,1,0:T(8,128)(2,1)}, bf16[128,80,128]{2,1,0:T(8,128)(2,1)S(1)}, u32[]{:S(2)}) copy-start(bf16[128,80,128]{2,1,0:T(8,128)(2,1)S(1)} %all-to-all-done.1.tail_hbm) | copy-start | bytes 7864324

commit v17 on v15

--- a/solution.py
+++ b/solution.py
@@ -8,7 +8,7 @@
 from jax.sharding import PartitionSpec as P
 
 MESH = pl.DeviceIdType.MESH
-CUT = 48
+CUT = 64
 
 
 def gather_kernel(n_nar, src_ref, pos_ref, dst_ref, pos_dst, send_sem, recv_sem, local_sem):

time: 146 us -> 146 us (level)
  the two profiles are of different devices: /device:TPU:152 before, /device:TPU:26 now
where the time goes in v17:
time: 146 us; the launch traced here: 145 us
  blocking collectives  70.6 us (48%)
  Pallas kernels  59.6 us (41%)
  starting transfers between devices  9.2 us (6%)
  waiting for transfers between devices  3.87 us (3%)
  local copies, waits for them, and re-layouts  2.04 us (1%)
    all_to_all x1, blocking collectives, on_device(): head = lax.all_to_all(head, 'wide', split_axis=0, concat_axis=0, tiled=True)  70.6 us
    pallas_call x1, Pallas kernels, gather_integrals(): pl.pallas_call(functools.partial(gather_kernel, n_nar), out_shape=(jax.Sh...  49.4 us
    all_to_all x1, starting transfers between devices, on_device(): tail = lax.all_to_all(tail, 'wide', split_axis=0, concat_axis=0, tiled=True)  9.2 us
    pallas_call x1, Pallas kernels, ladder(): pl.pallas_call(functools.partial(ladder_kernel, n_x, n_k, per), out_shape...  6.2 us
    pallas_call x1, Pallas kernels, pick_outgoing(): pl.pallas_call(functools.partial(pick_kernel, n_out, cut), out_shape=(jax...  3.99 us
    all_to_all x1, waiting for transfers between devices, on_device(): tail = lax.all_to_all(tail, 'wide', split_axis=0, concat_axis=0, tiled=True)  3.87 us
  transfers between devices with their start and end apart: 1, of which 1 were waited for; matrix products, arithmetic and copies ran while one was open for 0% of the time, Pallas kernels for 34%

profile of v17, /device:TPU:26, one launch (start us, length us, event | category | flops | bytes accessed | tf_op | source)
XLA Modules:
  0.0 145.3 jit_solution(6124332035534937714)
XLA Ops:
  0.0 4.0 %shard_map.47 = (bf16[128,64,128]{2,1,0:T(8,128)(2,1)}, bf16[128,64,128]{2,1,0:T(8,128)(2,1)}) custom-call(s32[128]{0:T(128)} %bitcast.1, bf16[16,128,128]{2,1,0:T(8,128)(2,1)} %amp_ref.1), custom_call_target="tpu_custom_call" | custom-call | bytes 8388608 | tf_op jit(solution)/shard_map/pallas_call | solution.py:148
  4.0 70.6 %all_to_all.10.head_hbm = bf16[128,64,128]{2,1,0:T(8,128)(2,1)} all-to-all(bf16[128,64,128]{2,1,0:T(8,128)(2,1)} %get-tuple-element.10), channel_id=1, replica_groups=mesh['wide'=64,'narrow'=8] {'wide'}, dimensions={0} | all-to-all | bytes 4194304 | tf_op jit(solution)/shard_map/all_to_all | solution.py:162
  74.6 0.0 copy-start.1
  74.6 9.2 %all-to-all-start.1 = ((bf16[128,64,128]{2,1,0:T(8,128)(2,1)}), bf16[128,64,128]{2,1,0:T(8,128)(2,1)S(1)}, u32[]{:S(2)}, u32[]{:S(2)}) async-start(bf16[128,64,128]{2,1,0:T(8,128)(2,1)} %get-tuple-element.11), calls=%async_computation.1 | async-start | bytes 4194304 | tf_op jit(solution)/shard_map/all_to_all | solution.py:163
  83.8 0.0 copy-done.1
  83.8 0.1 copy.5
  83.9 0.6 dynamic_update_slice.3.pos_ref
  84.5 49.4 %shard_map.46 = (bf16[8,8,2,128,128]{4,3,2,1,0:T(8,128)(2,1)}, s32[8,8,128]{2,1,0:T(8,128)}) custom-call(bf16[8,2,128,128]{3,2,1,0:T(8,128)(2,1)} %src_ref.1, s32[8,128]{1,0:T(8,128)} %dynamic_update_slice.3.pos_ref), custom_call_target="tpu_custom_call" | custom-call | bytes 8388608 | tf_op jit(solution)/shard_map/pallas_call | solution.py:58
  133.9 3.9 %all-to-all-done.1.tail_hbm = bf16[128,64,128]{2,1,0:T(8,128)(2,1)S(1)} async-done(((bf16[128,64,128]{2,1,0:T(8,128)(2,1)}), bf16[128,64,128]{2,1,0:T(8,128)(2,1)S(1)}, u32[]{:S(2)}, u32[]{:S(2)}) %all-to-all-start.1) | async-done | bytes 2097184 | tf_op jit(solution)/shard_map/all_to_all | solution.py:163
  137.8 0.0 copy-start
  137.8 1.3 copy-done
  139.1 6.2 %shard_map.48 = bf16[8,128,128]{2,1,0:T(8,128)(2,1)} custom-call(s32[8,8,128]{2,1,0:T(8,128)} %get-tuple-element.9.places_ref, bf16[128,64,128]{2,1,0:T(8,128)(2,1)} %all_to_all.10.head_hbm, bf16[128,64,128]{2,1,0:T(8,128)(2,1)} %copy-done, bf16[8,8,2,128,128]{4,3,2,1,0:T(8,128)(2,1)} %get-tuple-element.12.blk_hbm), custom_call_target="tpu_custom_call" | custom-call | flops 536870912 | bytes 8650752 | tf_op jit(solution)/shard_map/pallas_call | solution.py:111
Async XLA Ops:
  74.6 9.2 %copy-start.1 = (s32[8,2]{0,1:T(2,128)S(1)}, s32[8,2]{0,1:T(2,128)}, u32[]{:S(2)}) copy-start(s32[8,2]{0,1:T(2,128)} %param.6) | copy-start | bytes 196
  74.6 63.2 %all-to-all-start.1 = ((bf16[128,64,128]{2,1,0:T(8,128)(2,1)}), bf16[128,64,128]{2,1,0:T(8,128)(2,1)S(1)}, u32[]{:S(2)}, u32[]{:S(2)}) async-start(bf16[128,64,128]{2,1,0:T(8,128)(2,1)} %get-tuple-element.11), calls=%async_computation.1 | async-start | bytes 4194304 | tf_op jit(solution)/shard_map/all_to_all | solution.py:163
  137.8 1.4 copy-start

commit v18 on v15

--- a/solution.py
+++ b/solution.py
@@ -133,26 +133,42 @@
     )(places, head, tail, blocks)
 
 
-def pick_kernel(n_out, cut, sel_ref, amp_ref, head_ref, tail_ref):
+def pick_kernel(n_out, cut, n_chunks, sel_ref, amp_ref, head_hbm, tail_hbm, head_v, tail_v, sems):
+    size = n_out // n_chunks
+
     def body(j, carry):
         tile = amp_ref[sel_ref[j]]
-        head_ref[j] = tile[:cut]
-        tail_ref[j] = tile[cut:]
+        head_v[j] = tile[:cut]
+        tail_v[j] = tile[cut:]
         return carry
 
-    lax.fori_loop(0, n_out, body, 0)
+    copies = []
+    for c in range(n_chunks):
+        lax.fori_loop(c * size, (c + 1) * size, body, 0)
+        r = pl.ds(c * size, size)
+        for i, (v, h) in enumerate(((head_v, head_hbm), (tail_v, tail_hbm))):
+            copies.append(pltpu.make_async_copy(v.at[r], h.at[r], sems.at[i, c]))
+            copies[-1].start()
+    for cp in copies:
+        cp.wait()
 
 
 def pick_outgoing(amplitudes, selection, cut):
     n_out, (rows, t) = selection.shape[0], amplitudes.shape[1:]
+    n_chunks = 4
     return pl.pallas_call(
-        functools.partial(pick_kernel, n_out, cut),
+        functools.partial(pick_kernel, n_out, cut, n_chunks),
         out_shape=(
             jax.ShapeDtypeStruct((n_out, cut, t), amplitudes.dtype),
             jax.ShapeDtypeStruct((n_out, rows - cut, t), amplitudes.dtype),
         ),
         in_specs=[pl.BlockSpec(memory_space=pltpu.SMEM), pl.BlockSpec(memory_space=pltpu.VMEM)],
-        out_specs=(pl.BlockSpec(memory_space=pltpu.VMEM), pl.BlockSpec(memory_space=pltpu.VMEM)),
+        out_specs=(pl.BlockSpec(memory_space=pl.ANY), pl.BlockSpec(memory_space=pl.ANY)),
+        scratch_shapes=[
+            pltpu.VMEM((n_out, cut, t), amplitudes.dtype),
+            pltpu.VMEM((n_out, rows - cut, t), amplitudes.dtype),
+            pltpu.SemaphoreType.DMA((2, n_chunks)),
+        ],
         cost_estimate=pl.CostEstimate(flops=0, transcendentals=0, bytes_accessed=4 * n_out * amplitudes[0].size),
     )(selection, amplitudes)
 

time: 146 us -> 145 us (level)
  the two profiles are of different devices: /device:TPU:152 before, /device:TPU:158 now
where the time goes in v18:
time: 145 us
  Pallas kernels  58.2 us (40%)
  blocking collectives  55.1 us (38%)
  waiting for transfers between devices  20 us (14%)
  starting transfers between devices  8.98 us (6%)
  local copies, waits for them, and re-layouts  2.22 us (2%)
    all_to_all x1, blocking collectives, on_device(): head = lax.all_to_all(head, 'wide', split_axis=0, concat_axis=0, tiled=True)  55.1 us
    pallas_call x1, Pallas kernels, gather_integrals(): pl.pallas_call(functools.partial(gather_kernel, n_nar), out_shape=(jax.Sh...  48.7 us
    all_to_all x1, waiting for transfers between devices, on_device(): tail = lax.all_to_all(tail, 'wide', split_axis=0, concat_axis=0, tiled=True)  20 us
    all_to_all x1, starting transfers between devices, on_device(): tail = lax.all_to_all(tail, 'wide', split_axis=0, concat_axis=0, tiled=True)  8.98 us
    pallas_call x1, Pallas kernels, ladder(): pl.pallas_call(functools.partial(ladder_kernel, n_x, n_k, per), out_shape...  6.26 us
    pallas_call x1, Pallas kernels, pick_outgoing(): pl.pallas_call(functools.partial(pick_kernel, n_out, cut, n_chunks), out_...  3.3 us
  transfers between devices with their start and end apart: 1, of which 1 were waited for; matrix products, arithmetic and copies ran while one was open for 0% of the time, Pallas kernels for 34%

profile of v18, /device:TPU:158, one launch (start us, length us, event | category | flops | bytes accessed | tf_op | source)
XLA Modules:
  0.0 144.5 jit_solution(12530053270839206532)
XLA Ops:
  0.0 3.3 %shard_map.47 = (bf16[128,48,128]{2,1,0:T(8,128)(2,1)}, bf16[128,80,128]{2,1,0:T(8,128)(2,1)}) custom-call(s32[128]{0:T(128)} %bitcast.1, bf16[16,128,128]{2,1,0:T(8,128)(2,1)} %amp_ref.1), custom_call_target="tpu_custom_call" | custom-call | bytes 8388608 | tf_op jit(solution)/shard_map/pallas_call | solution.py:159
  3.3 55.1 %all_to_all.10.head_hbm = bf16[128,48,128]{2,1,0:T(8,128)(2,1)} all-to-all(bf16[128,48,128]{2,1,0:T(8,128)(2,1)} %get-tuple-element.10), channel_id=1, replica_groups=mesh['wide'=64,'narrow'=8] {'wide'}, dimensions={0} | all-to-all | bytes 3145728 | tf_op jit(solution)/shard_map/all_to_all | solution.py:178
  58.4 0.0 copy-start.1
  58.4 9.0 %all-to-all-start.1 = ((bf16[128,80,128]{2,1,0:T(8,128)(2,1)}), bf16[128,80,128]{2,1,0:T(8,128)(2,1)S(1)}, u32[]{:S(2)}, u32[]{:S(2)}) async-start(bf16[128,80,128]{2,1,0:T(8,128)(2,1)} %get-tuple-element.11), calls=%async_computation.1 | async-start | bytes 5242880 | tf_op jit(solution)/shard_map/all_to_all | solution.py:179
  67.3 0.0 copy-done.1
  67.4 0.1 copy.5
  67.4 0.6 dynamic_update_slice.3.pos_ref
  68.0 48.7 %shard_map.46 = (bf16[8,8,2,128,128]{4,3,2,1,0:T(8,128)(2,1)}, s32[8,8,128]{2,1,0:T(8,128)}) custom-call(bf16[8,2,128,128]{3,2,1,0:T(8,128)(2,1)} %src_ref.1, s32[8,128]{1,0:T(8,128)} %dynamic_update_slice.3.pos_ref), custom_call_target="tpu_custom_call" | custom-call | bytes 8388608 | tf_op jit(solution)/shard_map/pallas_call | solution.py:58
  116.7 20.0 %all-to-all-done.1.tail_hbm = bf16[128,80,128]{2,1,0:T(8,128)(2,1)S(1)} async-done(((bf16[128,80,128]{2,1,0:T(8,128)(2,1)}), bf16[128,80,128]{2,1,0:T(8,128)(2,1)S(1)}, u32[]{:S(2)}, u32[]{:S(2)}) %all-to-all-start.1) | async-done | bytes 2621472 | tf_op jit(solution)/shard_map/all_to_all | solution.py:179
  136.7 0.0 copy-start
  136.7 1.5 %copy-done = bf16[128,80,128]{2,1,0:T(8,128)(2,1)} copy-done((bf16[128,80,128]{2,1,0:T(8,128)(2,1)}, bf16[128,80,128]{2,1,0:T(8,128)(2,1)S(1)}, u32[]{:S(2)}) %copy-start) | copy-done | bytes 2621464
  138.2 6.3 %shard_map.48 = bf16[8,128,128]{2,1,0:T(8,128)(2,1)} custom-call(s32[8,8,128]{2,1,0:T(8,128)} %get-tuple-element.9.places_ref, bf16[128,48,128]{2,1,0:T(8,128)(2,1)} %all_to_all.10.head_hbm, bf16[128,80,128]{2,1,0:T(8,128)(2,1)} %copy-done, bf16[8,8,2,128,128]{4,3,2,1,0:T(8,128)(2,1)} %get-tuple-element.12.blk_hbm), custom_call_target="tpu_custom_call" | custom-call | flops 536870912 | bytes 8650752 | tf_op jit(solution)/shard_map/pallas_call | solution.py:111
Async XLA Ops:
  58.4 9.0 %copy-start.1 = (s32[8,2]{0,1:T(2,128)S(1)}, s32[8,2]{0,1:T(2,128)}, u32[]{:S(2)}) copy-start(s32[8,2]{0,1:T(2,128)} %param.6) | copy-start | bytes 196
  58.4 78.3 %all-to-all-start.1 = ((bf16[128,80,128]{2,1,0:T(8,128)(2,1)}), bf16[128,80,128]{2,1,0:T(8,128)(2,1)S(1)}, u32[]{:S(2)}, u32[]{:S(2)}) async-start(bf16[128,80,128]{2,1,0:T(8,128)(2,1)} %get-tuple-element.11), calls=%async_computation.1 | async-start | bytes 5242880 | tf_op jit(solution)/shard_map/all_to_all | solution.py:179
  136.7 1.5 %copy-start = (bf16[128,80,128]{2,1,0:T(8,128)(2,1)}, bf16[128,80,128]{2,1,0:T(8,128)(2,1)S(1)}, u32[]{:S(2)}) copy-start(bf16[128,80,128]{2,1,0:T(8,128)(2,1)S(1)} %all-to-all-done.1.tail_hbm) | copy-start | bytes 7864324

commit v19 on v18

--- a/solution.py
+++ b/solution.py
@@ -155,7 +155,7 @@
 
 def pick_outgoing(amplitudes, selection, cut):
     n_out, (rows, t) = selection.shape[0], amplitudes.shape[1:]
-    n_chunks = 4
+    n_chunks = 8
     return pl.pallas_call(
         functools.partial(pick_kernel, n_out, cut, n_chunks),
         out_shape=(

time: 145 us -> 145 us (level)
  the two profiles are of different devices: /device:TPU:158 before, /device:TPU:156 now
where the time goes in v19:
time: 145 us; the launch traced here: 144 us
  Pallas kernels  58 us (40%)
  blocking collectives  55.1 us (38%)
  waiting for transfers between devices  20.1 us (14%)
  starting transfers between devices  8.98 us (6%)
  local copies, waits for them, and re-layouts  2.22 us (2%)
    all_to_all x1, blocking collectives, on_device(): head = lax.all_to_all(head, 'wide', split_axis=0, concat_axis=0, tiled=True)  55.1 us
    pallas_call x1, Pallas kernels, gather_integrals(): pl.pallas_call(functools.partial(gather_kernel, n_nar), out_shape=(jax.Sh...  48.5 us
    all_to_all x1, waiting for transfers between devices, on_device(): tail = lax.all_to_all(tail, 'wide', split_axis=0, concat_axis=0, tiled=True)  20.1 us
    all_to_all x1, starting transfers between devices, on_device(): tail = lax.all_to_all(tail, 'wide', split_axis=0, concat_axis=0, tiled=True)  8.98 us
    pallas_call x1, Pallas kernels, ladder(): pl.pallas_call(functools.partial(ladder_kernel, n_x, n_k, per), out_shape...  6.25 us
    pallas_call x1, Pallas kernels, pick_outgoing(): pl.pallas_call(functools.partial(pick_kernel, n_out, cut, n_chunks), out_...  3.27 us
  transfers between devices with their start and end apart: 1, of which 1 were waited for; matrix products, arithmetic and copies ran while one was open for 0% of the time, Pallas kernels for 34%

profile of v19, /device:TPU:156, one launch (start us, length us, event | category | flops | bytes accessed | tf_op | source)
XLA Modules:
  0.0 144.5 jit_solution(2889389167065294860)
XLA Ops:
  0.0 3.3 %shard_map.47 = (bf16[128,48,128]{2,1,0:T(8,128)(2,1)}, bf16[128,80,128]{2,1,0:T(8,128)(2,1)}) custom-call(s32[128]{0:T(128)} %bitcast.1, bf16[16,128,128]{2,1,0:T(8,128)(2,1)} %amp_ref.1), custom_call_target="tpu_custom_call" | custom-call | bytes 8388608 | tf_op jit(solution)/shard_map/pallas_call | solution.py:159
  3.3 55.1 %all_to_all.10.head_hbm = bf16[128,48,128]{2,1,0:T(8,128)(2,1)} all-to-all(bf16[128,48,128]{2,1,0:T(8,128)(2,1)} %get-tuple-element.10), channel_id=1, replica_groups=mesh['wide'=64,'narrow'=8] {'wide'}, dimensions={0} | all-to-all | bytes 3145728 | tf_op jit(solution)/shard_map/all_to_all | solution.py:178
  58.3 0.0 copy-start.1
  58.3 9.0 %all-to-all-start.1 = ((bf16[128,80,128]{2,1,0:T(8,128)(2,1)}), bf16[128,80,128]{2,1,0:T(8,128)(2,1)S(1)}, u32[]{:S(2)}, u32[]{:S(2)}) async-start(bf16[128,80,128]{2,1,0:T(8,128)(2,1)} %get-tuple-element.11), calls=%async_computation.1 | async-start | bytes 5242880 | tf_op jit(solution)/shard_map/all_to_all | solution.py:179
  67.3 0.0 copy-done.1
  67.3 0.1 copy.5
  67.4 0.6 dynamic_update_slice.3.pos_ref
  68.0 48.5 %shard_map.46 = (bf16[8,8,2,128,128]{4,3,2,1,0:T(8,128)(2,1)}, s32[8,8,128]{2,1,0:T(8,128)}) custom-call(bf16[8,2,128,128]{3,2,1,0:T(8,128)(2,1)} %src_ref.1, s32[8,128]{1,0:T(8,128)} %dynamic_update_slice.3.pos_ref), custom_call_target="tpu_custom_call" | custom-call | bytes 8388608 | tf_op jit(solution)/shard_map/pallas_call | solution.py:58
  116.5 20.1 %all-to-all-done.1.tail_hbm = bf16[128,80,128]{2,1,0:T(8,128)(2,1)S(1)} async-done(((bf16[128,80,128]{2,1,0:T(8,128)(2,1)}), bf16[128,80,128]{2,1,0:T(8,128)(2,1)S(1)}, u32[]{:S(2)}, u32[]{:S(2)}) %all-to-all-start.1) | async-done | bytes 2621472 | tf_op jit(solution)/shard_map/all_to_all | solution.py:179
  136.7 0.0 copy-start
  136.7 1.5 %copy-done = bf16[128,80,128]{2,1,0:T(8,128)(2,1)} copy-done((bf16[128,80,128]{2,1,0:T(8,128)(2,1)}, bf16[128,80,128]{2,1,0:T(8,128)(2,1)S(1)}, u32[]{:S(2)}) %copy-start) | copy-done | bytes 2621464
  138.2 6.3 %shard_map.48 = bf16[8,128,128]{2,1,0:T(8,128)(2,1)} custom-call(s32[8,8,128]{2,1,0:T(8,128)} %get-tuple-element.9.places_ref, bf16[128,48,128]{2,1,0:T(8,128)(2,1)} %all_to_all.10.head_hbm, bf16[128,80,128]{2,1,0:T(8,128)(2,1)} %copy-done, bf16[8,8,2,128,128]{4,3,2,1,0:T(8,128)(2,1)} %get-tuple-element.12.blk_hbm), custom_call_target="tpu_custom_call" | custom-call | flops 536870912 | bytes 8650752 | tf_op jit(solution)/shard_map/pallas_call | solution.py:111
Async XLA Ops:
  58.3 9.0 %copy-start.1 = (s32[8,2]{0,1:T(2,128)S(1)}, s32[8,2]{0,1:T(2,128)}, u32[]{:S(2)}) copy-start(s32[8,2]{0,1:T(2,128)} %param.6) | copy-start | bytes 196
  58.3 78.3 %all-to-all-start.1 = ((bf16[128,80,128]{2,1,0:T(8,128)(2,1)}), bf16[128,80,128]{2,1,0:T(8,128)(2,1)S(1)}, u32[]{:S(2)}, u32[]{:S(2)}) async-start(bf16[128,80,128]{2,1,0:T(8,128)(2,1)} %get-tuple-element.11), calls=%async_computation.1 | async-start | bytes 5242880 | tf_op jit(solution)/shard_map/all_to_all | solution.py:179
  136.7 1.5 %copy-start = (bf16[128,80,128]{2,1,0:T(8,128)(2,1)}, bf16[128,80,128]{2,1,0:T(8,128)(2,1)S(1)}, u32[]{:S(2)}) copy-start(bf16[128,80,128]{2,1,0:T(8,128)(2,1)S(1)} %all-to-all-done.1.tail_hbm) | copy-start | bytes 7864324
